TPU v7x, 32 devices: a whole 2x2x4 slice. The times are simulated.
32 devices in a mesh: dp: 16 (over z, x, core), head: 2 (over y).
Axes of the slice: x: 2, y: 2, z: 4, core: 2. Of those that a mesh axis runs over, the one named last changes fastest.
Arguments:
- inputs: bfloat16 [16384, 768], P(('dp', 'head')), may hold values from -6 to 6
- lengths: int32 [32], P('dp'), may hold values from 16 to 512, as said below
- labels: int32 [32], P(('dp', 'head')), may hold values from 0 to 2
- state_cotangent: bfloat16 [16384, 768], P(('dp', 'head')), may hold values from -6 to 6
- query_weight: bfloat16 [768, 768], P(None, 'head'), may hold values from -0.4375 to 0.4375
- query_bias: bfloat16 [768], P('head'), may hold values from -4 to 4
- key_weight: bfloat16 [768, 768], P(None, 'head'), may hold values from -0.21875 to 0.21875
- value_weight: bfloat16 [768, 768], P(None, 'head'), may hold values from -0.21875 to 0.21875
- value_bias: bfloat16 [768], P('head'), may hold values from -4 to 4
- out_weight: bfloat16 [768, 768], replicated, may hold values from -0.625 to 0.625
- out_bias: bfloat16 [768], replicated, may hold values from -4 to 4
- first_gain: bfloat16 [768], replicated, may hold values from 0.5 to 1.5
- first_shift: bfloat16 [768], replicated, may hold values from -4 to 4
- up_weight: bfloat16 [768, 3072], replicated, may hold values from -0.21875 to 0.21875
- up_bias: bfloat16 [3072], replicated, may hold values from -4 to 4
- down_weight: bfloat16 [3072, 768], replicated, may hold values from -0.15625 to 0.15625
- down_bias: bfloat16 [768], replicated, may hold values from -4 to 4
- second_gain: bfloat16 [768], replicated, may hold values from 0.5 to 1.5
- second_shift: bfloat16 [768], replicated, may hold values from -4 to 4
- pool_weight: bfloat16 [768, 768], replicated, may hold values from -0.21875 to 0.21875
- pool_bias: bfloat16 [768], replicated, may hold values from -4 to 4
- class_weight: bfloat16 [768, 3], replicated, may hold values from -0.875 to 0.875
- class_bias: bfloat16 [3], replicated, may hold values from -4 to 4
Outputs:
- states: bfloat16 [16384, 768], P(('dp', 'head'))
- input_grad: bfloat16 [16384, 768], P(('dp', 'head'))
- logits: float32 [32, 3], P(('dp', 'head'))
- loss: float32 [], replicated
- query_weight_grad: float32 [768, 768], P('dp', 'head')
- query_bias_grad: float32 [768], P('head')
- key_weight_grad: float32 [768, 768], P('dp', 'head')
- value_weight_grad: float32 [768, 768], P('dp', 'head')
- value_bias_grad: float32 [768], P('head')
- out_weight_grad: float32 [768, 768], P('dp', 'head')
- out_bias_grad: float32 [768], replicated
- first_gain_grad: float32 [768], replicated
- first_shift_grad: float32 [768], replicated
- up_weight_grad: float32 [768, 3072], P('dp', 'head')
- up_bias_grad: float32 [3072], replicated
- down_weight_grad: float32 [3072, 768], P('dp', 'head')
- down_bias_grad: float32 [768], replicated
- second_gain_grad: float32 [768], replicated
- second_shift_grad: float32 [768], replicated
- pool_weight_grad: float32 [768, 768], P('dp', 'head')
- pool_bias_grad: float32 [768], replicated
- class_weight_grad: float32 [768, 3], replicated
- class_bias_grad: float32 [3], replicated
Inputs may be any that keep to these rules, and one draw needn't show every extreme that they name: `lengths`: every sequence has at least one real token; some sequence is full and some has the fewest.
All inputs are finite; a program needn't handle non-finite values.
Results may differ from a plain program's by a relative error of at most 0.015.
The roundings to bfloat16 on the way count: a program that leaves them out, or rounds other values in their place, can miss the bound.
Values may be sent and summed in bfloat16 or wider, within the bound.
A program may use at most 192 MiB of HBM per device.

v0:
```python
from functools import partial

import jax
import jax.numpy as jnp
from jax import lax
from jax.experimental import pallas as pl
from jax.experimental.pallas import tpu as pltpu
from jax.sharding import PartitionSpec as P

HEAD_DIM = 64
SEQ_LEN = 512
NEGATIVE = -1e30
EPSILON = 1e-06
MESH = pl.DeviceIdType.MESH
F32 = jnp.float32
BF16 = jnp.bfloat16
VMEM_LIMIT = 62 << 20


def normalize(values, gain, shift):
    center = values - jnp.mean(values, -1, keepdims=True)
    spread = jnp.mean(center * center, -1, keepdims=True)
    return center * lax.rsqrt(spread + EPSILON) * gain + shift


def matmul(left, right):
    return jnp.dot(left, right, preferred_element_type=F32)


def column_sums(values):
    return jnp.sum(values.astype(F32), 0)


class Place:
    def __init__(self, bits):
        self.bits = bits
        self.dp = lax.axis_index("dp")
        self.head = lax.axis_index("head")
        self.mine = [lax.rem(self.dp // (1 << b), 2) for b in range(bits - 1)] + [self.head]

    def partner(self, bit):
        if bit == self.bits - 1:
            return (self.dp, 1 - self.head)
        return (self.dp + (1 - 2 * self.mine[bit]) * (1 << bit), self.head)

    def greet(self, bits):
        barrier = pltpu.get_barrier_semaphore()
        for bit in bits:
            pl.semaphore_signal(barrier, inc=1, device_id=self.partner(bit), device_id_type=MESH)
        pl.semaphore_wait(barrier, len(bits))


def shared_rows(bits):
    return 1, 2


def lane_iota(shape):
    return lax.broadcasted_iota(jnp.int32, shape, 1)


def first_lanes(shape):
    return lane_iota(shape) < HEAD_DIM


def pair_operands(q2, k2, length, parity):
    lanes = lane_iota(q2.shape)
    rows = lax.broadcasted_iota(jnp.int32, q2.shape, 0)
    mine = (lanes < HEAD_DIM) if parity == 0 else (lanes >= HEAD_DIM)
    spare = lanes == (HEAD_DIM if parity == 0 else 0)
    hidden = jnp.where(rows < length, 0.0, NEGATIVE)
    qa = jnp.where(mine, q2.astype(F32) * HEAD_DIM ** -0.5, jnp.where(spare, 1.0, 0.0)).astype(BF16)
    ka = jnp.where(mine, k2.astype(F32), jnp.where(spare, hidden, 0.0)).astype(BF16)
    return qa, ka


def nt(left, right):
    return lax.dot_general(left, right, (((1,), (1,)), ((), ())), preferred_element_type=F32)


def tn(left, right):
    return lax.dot_general(left, right, (((0,), (0,)), ((), ())), preferred_element_type=F32)


def attend_pair(q_ref, k_ref, v_ref, ctx_ref, lse_ref, pair, length):
    at = pl.ds(pl.multiple_of(pair * 128, 128), 128)
    q2, k2, v2 = q_ref[:, at], k_ref[:, at], v_ref[:, at]
    v2t = v2.T
    rows = lax.broadcasted_iota(jnp.int32, (128, SEQ_LEN), 0)
    parts = []
    for parity in range(2):
        qa, ka = pair_operands(q2, k2, length, parity)
        scores = nt(ka, qa)
        peak = jnp.max(scores, 0, keepdims=True)
        raised = jnp.exp(scores - peak)
        total = jnp.sum(raised, 0, keepdims=True)
        probs = (raised * (1.0 / total)).astype(BF16)
        parts.append(matmul(v2t, probs))
        lse_ref[pair, parity : parity + 1, :] = peak + jnp.log(total)
    joined = jnp.where(rows < HEAD_DIM, parts[0], parts[1])
    ctx_ref[:, at] = joined.T.astype(BF16)


def attention_forward(inputs, weights, biases, lengths, bits):
    rows, width = inputs.shape
    depth, half = weights[0].shape
    part = depth // 8
    pairs = half // 128
    kinds = 10

    def kernel(lengths_ref, x_ref, wq_ref, wk_ref, wv_ref, bias_ref, q_ref, k_ref, v_ref, ctx_ref, lse_ref, fq_ref,
               fk_ref, fv_ref, bias_got, send, recv, bias_send, bias_recv):
        place = Place(bits)
        head = place.head
        bit_x, bit_z = shared_rows(bits)
        place.greet([0, bit_x, bit_z, bits - 1])
        length = lengths_ref[head]
        own_refs, full_refs = (wq_ref, wk_ref, wv_ref), (fq_ref, fk_ref, fv_ref)
        own = pl.ds(pl.multiple_of(head * half, half), half)
        other = pl.ds(pl.multiple_of((1 - head) * half, half), half)
        core, x, z = place.mine[0], place.mine[bit_x], place.mine[bit_z]

        def rows_of(at_x, at_z, lower=None):
            start = core * (4 * part) + (at_z * 2 + at_x) * part
            if lower is None:
                return pl.ds(pl.multiple_of(start, part), part)
            return pl.ds(pl.multiple_of(start + lower * (part // 2), part // 2), part // 2)

        started = {}

        def start(j, kind, source, where, bit):
            copy = pltpu.make_async_remote_copy(
                src_ref=source, dst_ref=full_refs[j].at[where], send_sem=send.at[j, kind], recv_sem=recv.at[j, kind],
                device_id=place.partner(bit), device_id_type=MESH)
            copy.start()
            started[j, kind] = copy

        bias_copy = pltpu.make_async_remote_copy(
            src_ref=bias_ref, dst_ref=bias_got, send_sem=bias_send, recv_sem=bias_recv,
            device_id=place.partner(bits - 1), device_id_type=MESH)
        for j in range(3):
            mine = rows_of(x, z)
            start(j, 0, own_refs[j].at[mine, :], (mine, own), bits - 1)
        bias_copy.start()

        def forward(j, kind, where, bit):
            start(j, kind, full_refs[j].at[where], where, bit)

        def stage_one(j):
            started[j, 0].wait_recv()
            where = (rows_of(x, z), other)
            forward(j, 1, where, bit_x)
            forward(j, 2, where, bit_z)
            forward(j, 5, where, 0)

        def stage_two(j):
            started[j, 1].wait_recv()
            forward(j, 4, (rows_of(1 - x, z, 1), other), bit_z)
            forward(j, 6, (rows_of(1 - x, z), other), 0)
            started[j, 2].wait_recv()
            forward(j, 3, (rows_of(x, 1 - z, 0), other), bit_x)
            forward(j, 7, (rows_of(x, 1 - z), other), 0)

        def stage_three(j):
            for kind, lower in ((3, 0), (4, 1)):
                started[j, kind].wait_recv()
                forward(j, kind + 5, (rows_of(1 - x, 1 - z, lower), other), 0)

        def stage_four(j):
            for kind in range(5, 10):
                started[j, kind].wait_recv()

        def project(j, where, bias):
            value = matmul(x_ref[...], full_refs[j][:, where])
            if bias is not None:
                value = value + bias
            (q_ref, k_ref, v_ref)[j][:, where] = value.astype(BF16)

        for j in range(3):
            full_refs[j][:, own] = own_refs[j][...]
        project(0, own, bias_ref[0:1, :])
        project(1, own, None)
        project(2, own, bias_ref[1:2, :])

        def attend(pair):
            attend_pair(q_ref, k_ref, v_ref, ctx_ref, lse_ref, pair, length)

        stage_one(0)
        attend(head * pairs)
        stage_one(1)
        stage_two(0)
        attend(head * pairs + 1)
        stage_one(2)
        stage_two(1)
        stage_three(0)
        attend(head * pairs + 2)
        stage_two(2)
        stage_three(1)
        stage_three(2)
        bias_copy.wait_recv()
        stage_four(0)
        project(0, other, bias_got[0:1, :])
        stage_four(1)
        project(1, other, None)
        stage_four(2)
        project(2, other, bias_got[1:2, :])

        def late(n, carry):
            attend((1 - head) * pairs + n)
            return carry

        lax.fori_loop(0, pairs, late, 0)
        for copy in started.values():
            copy.wait_send()
        bias_copy.wait_send()

    vmem = pl.BlockSpec(memory_space=pltpu.VMEM)
    act = jax.ShapeDtypeStruct((rows, width), BF16)
    full = jax.ShapeDtypeStruct((depth, width), BF16)
    return pl.pallas_call(
        kernel,
        out_shape=[act] * 4 + [jax.ShapeDtypeStruct((2 * pairs, 2, rows), F32)] + [full] * 3,
        in_specs=[pl.BlockSpec(memory_space=pltpu.SMEM)] + [vmem] * 5,
        out_specs=[vmem] * 8,
        scratch_shapes=[pltpu.VMEM(biases.shape, F32), pltpu.SemaphoreType.DMA((3, kinds)),
                        pltpu.SemaphoreType.DMA((3, kinds)), pltpu.SemaphoreType.DMA, pltpu.SemaphoreType.DMA],
        compiler_params=pltpu.CompilerParams(collective_id=0, has_side_effects=True, vmem_limit_bytes=VMEM_LIMIT),
        name="attention_forward",
    )(lengths, inputs, *weights, biases)


def gelu_parts(v):
    x = jnp.abs(v) * 0.7071067811865476
    t = 1.0 / (1.0 + 0.3275911 * x)
    bell = jnp.exp(-0.5 * (v * v))
    tail = 0.5 * bell * t * (
        0.254829592 + t * (-0.284496736 + t * (1.421413741 + t * (-1.453152027 + t * 1.061405429))))
    phi = jnp.where(v >= 0, 1.0 - tail, tail)
    return v * phi, phi + v * bell * 0.3989422804014327


ROW_BLOCK = 64


def over_rows(rows, step, carry):
    def one(n, kept):
        return step(pl.ds(pl.multiple_of(n * ROW_BLOCK, ROW_BLOCK), ROW_BLOCK), kept)

    return lax.fori_loop(0, rows // ROW_BLOCK, one, carry)


OUT_BIAS, FIRST_GAIN, FIRST_SHIFT, DOWN_BIAS, SECOND_GAIN, SECOND_SHIFT, POOL_BIAS, CLASS_BIAS, UP_BIAS = range(9)
QUERY_BIAS, VALUE_BIAS, LOSS = 6, 7, 12


def row_side(context, inputs, cotangent, vectors, class_padded, labels, out_weight, up_weight, down_weight, pool_weight,
             devices, head_size):
    rows, width = inputs.shape
    hidden = up_weight.shape[1]
    half = width // 2
    chunk = half
    chunks = hidden // chunk
    times = hidden // width
    dp_size = devices // head_size
    block = width // dp_size
    classes_padded = class_padded.shape[1]
    per_width = width // 128

    def kernel(labels_ref, ctx_ref, x_ref, vec_ref, cls_ref, ow_ref, cot_hbm, up_hbm, down_hbm, pool_hbm,
               states_ref, gfirst_ref, gctx_ref, small_ref, fact_ref, logit_ref, up_out, down_out, out_out,
               cot, up_w, down_w, pool_w, first, low_ref, n1, r1, n2, r2, hid, slope, acc, gb_ref, ga_ref,
               frow, up_buf, down_buf, out_buf, load_sem, store_sem):
        loads = []
        for i, (source, target) in enumerate(
            ((up_hbm, up_w), (down_hbm, down_w), (pool_hbm, pool_w), (cot_hbm, cot))):
            load = pltpu.make_async_copy(source, target, load_sem.at[i])
            load.start()
            loads.append(load)

        def vec(i):
            return vec_ref[i : i + 1, :]

        acc[...] = matmul(ctx_ref[...], ow_ref[...])

        def norm_one(at, carry):
            value = x_ref[at, :].astype(F32) + (acc[at, :] + vec(OUT_BIAS))
            center = value - jnp.mean(value, -1, keepdims=True)
            scale = lax.rsqrt(jnp.mean(center * center, -1, keepdims=True) + EPSILON)
            normal = center * scale
            out = normal * vec(FIRST_GAIN) + vec(FIRST_SHIFT)
            n1[at, :] = normal
            r1[at, :] = scale
            first[at, :] = out
            low_ref[at, :] = out.astype(BF16)
            acc[at, :] = jnp.zeros_like(out)
            return carry

        over_rows(rows, norm_one, 0)
        loads[0].wait()
        loads[1].wait()

        def forward(c, carry):
            at = pl.ds(pl.multiple_of(c * chunk, chunk), chunk)
            pre = matmul(low_ref[...], up_w[:, at]) + vec_ref[pl.ds(UP_BIAS + c // 2, 1), pl.ds(pl.multiple_of(lax.rem(c, 2) * half, half), half)]
            act, deriv = gelu_parts(pre)
            act = act.astype(BF16)
            hid[:, at] = act
            slope[:, at] = deriv
            acc[...] += matmul(act, down_w[at, :])
            return carry

        lax.fori_loop(0, chunks, forward, 0)

        def norm_two(at, carry):
            value = first[at, :] + (acc[at, :] + vec(DOWN_BIAS))
            center = value - jnp.mean(value, -1, keepdims=True)
            scale = lax.rsqrt(jnp.mean(center * center, -1, keepdims=True) + EPSILON)
            normal = center * scale
            n2[at, :] = normal
            r2[at, :] = scale
            states_ref[at, :] = (normal * vec(SECOND_GAIN) + vec(SECOND_SHIFT)).astype(BF16)
            return carry

        over_rows(rows, norm_two, 0)

        loads[2].wait()
        loads[3].wait()
        lead = states_ref[0:16, :]
        pooled = jnp.tanh(matmul(lead, pool_w[...]) + vec(POOL_BIAS))
        pooled_low = pooled.astype(BF16)
        logits = matmul(pooled_low, cls_ref[...]) + vec_ref[CLASS_BIAS : CLASS_BIAS + 1, 0:classes_padded]
        lanes = lane_iota(logits.shape)
        logits = jnp.where(lanes < 3, logits, NEGATIVE)
        top = jnp.max(logits, -1, keepdims=True)
        norm = top + jnp.log(jnp.sum(jnp.exp(logits - top), -1, keepdims=True))
        target = jnp.where(lanes == labels_ref[0], 1.0, 0.0)
        loss = (norm - jnp.sum(jnp.where(lanes < 3, target * logits, 0.0), -1, keepdims=True)) / devices
        grad_logits = (jnp.where(lanes < 3, jnp.exp(logits - norm) - target, 0.0) / devices).astype(BF16)
        grad_pooled = (nt(grad_logits, cls_ref[...]) * (1.0 - pooled * pooled)).astype(BF16)
        grad_lead = nt(grad_pooled, pool_w[...])
        logit_ref[...] = logits[0:8, :]
        frow[...] = jnp.zeros_like(frow)
        for k, value in enumerate((lead, grad_pooled, pooled_low)):
            wide = value.astype(F32)
            for j in range(per_width):
                frow[k * per_width + j : k * per_width + j + 1, :] = wide[0:1, j * 128 : (j + 1) * 128]
        frow[3 * per_width : 3 * per_width + 1, :] = grad_logits.astype(F32)[0:1, 0:128]
        fact_ref[...] = frow[...].astype(BF16)

        def back_two(at, sums):
            gain_sum, shift_sum, bias_sum = sums
            row = at.start + lax.broadcasted_iota(jnp.int32, (ROW_BLOCK, width), 0)
            grad = cot[at, :].astype(F32) + jnp.where(row == 0, grad_lead[0:1, :], 0.0)
            normal = n2[at, :]
            e = grad * vec(SECOND_GAIN)
            value = (e - jnp.mean(e, -1, keepdims=True) - normal * jnp.mean(e * normal, -1, keepdims=True)) * r2[at, :]
            rounded = value.astype(BF16)
            acc[at, :] = value
            gb_ref[at, :] = rounded
            return (gain_sum + jnp.sum(grad * normal, 0, keepdims=True), shift_sum + jnp.sum(grad, 0, keepdims=True),
                    bias_sum + jnp.sum(rounded.astype(F32), 0, keepdims=True))

        zero = jnp.zeros((1, width), F32)
        gain_sum, shift_sum, bias_sum = over_rows(rows, back_two, (zero, zero, zero))
        small_ref[...] = jnp.zeros_like(small_ref)
        small_ref[SECOND_GAIN : SECOND_GAIN + 1, :] = gain_sum
        small_ref[SECOND_SHIFT : SECOND_SHIFT + 1, :] = shift_sum
        small_ref[DOWN_BIAS : DOWN_BIAS + 1, :] = bias_sum
        small_ref[LOSS : LOSS + 1, :] = jnp.broadcast_to(loss[0:1, 0:1], (1, width))

        def stores_of(c):
            slot = lax.rem(c, 2)
            up = pltpu.make_async_copy(up_buf.at[slot], up_out.at[lax.rem(c, times), c // times], store_sem.at[0, slot])
            down = pltpu.make_async_copy(
                down_buf.at[slot], down_out.at[:, :, pl.ds(c * (chunk // (times * block)), chunk // (times * block))],
                store_sem.at[1, slot])
            return up, down

        def backward(c, carry):
            at = pl.ds(pl.multiple_of(c * chunk, chunk), chunk)
            slot = lax.rem(c, 2)
            grad = (nt(gb_ref[...], down_w[at, :]) * slope[:, at]).astype(BF16)
            small_ref[pl.ds(UP_BIAS + c // 2, 1), pl.ds(pl.multiple_of(lax.rem(c, 2) * half, half), half)] = jnp.sum(
                grad.astype(F32), 0, keepdims=True)

            @pl.when(c >= 2)
            def _():
                for copy in stores_of(c - 2):
                    copy.wait()

            up_buf[slot] = tn(low_ref[...], grad).astype(BF16).reshape(dp_size, block, half)
            wide = tn(hid[:, at], gb_ref[...]).astype(BF16).reshape(chunk // (times * block), times, block, width)
            for t in range(times):
                for h in range(2):
                    down_buf[slot, t, h] = wide[:, t, :, h * half : (h + 1) * half]
            for copy in stores_of(c):
                copy.start()
            acc[...] += nt(grad, up_w[:, at])
            return carry

        lax.fori_loop(0, chunks, backward, 0)

        def back_one(at, sums):
            gain_sum, shift_sum, bias_sum = sums
            grad = acc[at, :]
            normal = n1[at, :]
            e = grad * vec(FIRST_GAIN)
            value = (e - jnp.mean(e, -1, keepdims=True) - normal * jnp.mean(e * normal, -1, keepdims=True)) * r1[at, :]
            rounded = value.astype(BF16)
            gfirst_ref[at, :] = value
            ga_ref[at, :] = rounded
            return (gain_sum + jnp.sum(grad * normal, 0, keepdims=True), shift_sum + jnp.sum(grad, 0, keepdims=True),
                    bias_sum + jnp.sum(rounded.astype(F32), 0, keepdims=True))

        gain_sum, shift_sum, bias_sum = over_rows(rows, back_one, (zero, zero, zero))
        small_ref[FIRST_GAIN : FIRST_GAIN + 1, :] = gain_sum
        small_ref[FIRST_SHIFT : FIRST_SHIFT + 1, :] = shift_sum
        small_ref[OUT_BIAS : OUT_BIAS + 1, :] = bias_sum
        gctx_ref[...] = nt(ga_ref[...], ow_ref[...]).astype(BF16)
        grad_out = tn(ctx_ref[...], ga_ref[...]).astype(BF16).reshape(dp_size, block, width)
        for h in range(2):
            out_buf[h] = grad_out[:, :, h * half : (h + 1) * half]
        out_copy = pltpu.make_async_copy(out_buf, out_out, store_sem.at[2, 0])
        out_copy.start()
        for c in range(chunks - 2, chunks):
            for copy in stores_of(c):
                copy.wait()
        out_copy.wait()

    vmem = pl.BlockSpec(memory_space=pltpu.VMEM)
    anywhere = pl.BlockSpec(memory_space=pl.ANY)
    act_low, act = jax.ShapeDtypeStruct((rows, width), BF16), jax.ShapeDtypeStruct((rows, width), F32)
    pieces = jax.ShapeDtypeStruct((times, 2, dp_size, block, half), BF16)
    fact_rows = -(-(3 * per_width + 1) // 16) * 16
    return pl.pallas_call(
        kernel,
        out_shape=[
            act_low, act, act_low, jax.ShapeDtypeStruct((16, width), F32), jax.ShapeDtypeStruct((fact_rows, 128), BF16),
            jax.ShapeDtypeStruct((8, classes_padded), F32), pieces, pieces,
            jax.ShapeDtypeStruct((2, dp_size, block, half), BF16),
        ],
        in_specs=[pl.BlockSpec(memory_space=pltpu.SMEM)] + [vmem] * 5 + [anywhere] * 4,
        out_specs=[vmem] * 6 + [anywhere] * 3,
        scratch_shapes=[
            pltpu.VMEM((rows, width), BF16),
            pltpu.VMEM((width, hidden), BF16),
            pltpu.VMEM((hidden, width), BF16),
            pltpu.VMEM((width, width), BF16),
            pltpu.VMEM((rows, width), F32),
            pltpu.VMEM((rows, width), BF16),
            pltpu.VMEM((rows, width), F32),
            pltpu.VMEM((rows, 1), F32),
            pltpu.VMEM((rows, width), F32),
            pltpu.VMEM((rows, 1), F32),
            pltpu.VMEM((rows, hidden), BF16),
            pltpu.VMEM((rows, hidden), F32),
            pltpu.VMEM((rows, width), F32),
            pltpu.VMEM((rows, width), BF16),
            pltpu.VMEM((rows, width), BF16),
            pltpu.VMEM((fact_rows, 128), F32),
            pltpu.VMEM((2, dp_size, block, half), BF16),
            pltpu.VMEM((2, times, 2, chunk // (times * block), block, half), BF16),
            pltpu.VMEM((2, dp_size, block, half), BF16),
            pltpu.SemaphoreType.DMA((4,)),
            pltpu.SemaphoreType.DMA((3, 2)),
        ],
        compiler_params=pltpu.CompilerParams(vmem_limit_bytes=VMEM_LIMIT),
        name="row_side",
    )(labels, context, inputs, vectors, class_padded, out_weight, cotangent, up_weight, down_weight, pool_weight)


def orders(bits):
    head = bits - 1
    rest = list(range(2, head))
    return [[0, 1, head] + rest, [0, head, 1] + rest, [0] + rest[:1] + [1, head] + rest[1:]]


def attention_backward(queries, keys, values, grad_context, inputs, full, grad_first, log_totals, lengths, up_pieces,
                       down_pieces, out_piece, small, factors, bits):
    times, _, dp_size, block, half = up_pieces.shape
    rows, width = inputs.shape
    plans = orders(bits)
    group = len(plans)
    count = 2 * times + 4
    groups = count // group
    grid_dims = (2,) * bits
    stages = bits
    head = bits - 1
    small_order = [0, 1, head] + list(range(2, head))
    pairs = width // 128

    def kernel(lengths_ref, q_ref, k_ref, v_ref, gc_ref, x_ref, wq_ref, wk_ref, wv_ref, gfirst_ref, lse_ref, small_in,
               factor_in, up_in, down_in, out_in, grad_ref, sums_ref, small_out, factor_out, held, *rest):
        got = rest[:stages]
        (dq_ref, dk_ref, dv_ref, small_buf, small_got, load_sem, send, recv, side_send, side_recv) = rest[stages:]
        place = Place(bits)
        loads = []
        sources = [up_in.at[i] for i in range(times)] + [down_in.at[i] for i in range(times)] + [out_in]
        for i, source in enumerate(sources):
            load = pltpu.make_async_copy(source, held.at[i], load_sem.at[i])
            load.start()
            loads.append(load)
        slot = sum(place.mine[bit] * (1 << k) for k, bit in enumerate(small_order))
        factor_out[slot] = factor_in[...]
        place.greet(range(bits))
        length = lengths_ref[place.head]

        def index(i, done, fixed, free_bits):
            out = [i]
            for bit in reversed(range(bits)):
                if bit in fixed:
                    out.append(fixed[bit])
                elif bit in done:
                    out.append(place.mine[bit])
                else:
                    out.append(free_bits[bit] if free_bits is not None else slice(None))
            return tuple(out)

        started = {}

        def send_piece(i, s):
            plan = plans[i % group]
            bit = plan[s]
            source = held.at[index(i, plan[:s], {bit: 1 - place.mine[bit]}, None)]
            copy = pltpu.make_async_remote_copy(
                src_ref=source, dst_ref=got[s].at[i], send_sem=send.at[i, s], recv_sem=recv.at[i, s],
                device_id=place.partner(bit), device_id_type=MESH)
            copy.start()
            started[i, s] = copy

        def add_piece(i, s):
            started[i, s].wait_recv()
            done = plans[i % group][: s + 1]
            free = [bit for bit in reversed(range(bits)) if bit not in done]
            if not free:
                where = index(i, done, {}, None)
                sums_ref[i] = held[where].astype(F32) + got[s][i].astype(F32)
                return

            def step(n, carry):
                free_bits = {bit: lax.rem(n // (1 << (len(free) - 1 - k)), 2) for k, bit in enumerate(free)}
                where = index(i, done, {}, free_bits)
                there = (i,) + tuple(free_bits[bit] for bit in free)
                held[where] = (held[where].astype(F32) + got[s][there].astype(F32)).astype(BF16)
                return carry

            lax.fori_loop(0, 1 << len(free), step, 0)

        def advance(g, s):
            for i in range(g * group, (g + 1) * group):
                if s == 0:
                    if i < len(loads):
                        loads[i].wait()
                else:
                    add_piece(i, s - 1)
                if s < stages:
                    send_piece(i, s)

        def side_send_stage(s):
            partner = place.partner(small_order[s])
            copies = []
            start = (slot // (1 << s)) * (1 << s)
            rows_at = pl.ds(start, 1 << s)
            for k, (source, target) in enumerate(
                ((small_buf.at[s], small_got.at[s]), (factor_out.at[rows_at], factor_out.at[rows_at]))
            ):
                copy = pltpu.make_async_remote_copy(
                    src_ref=source, dst_ref=target, send_sem=side_send.at[k, s], recv_sem=side_recv.at[k, s],
                    device_id=partner, device_id_type=MESH)
                copy.start()
                copies.append(copy)
            started["side", s] = copies

        def side_add_stage(s):
            for copy in started["side", s]:
                copy.wait_recv()
            total = small_buf[s] + small_got[s]
            if s < stages - 1:
                small_buf[s + 1] = total
            else:
                small_out[...] = total

        lanes_row = lax.broadcasted_iota(jnp.int32, (128, rows), 0)
        lanes = lane_iota((rows, 128))

        def attend(pair, carry):
            at = pl.ds(pl.multiple_of(pair * 128, 128), 128)
            q2, k2, v2, g2 = q_ref[:, at], k_ref[:, at], v_ref[:, at], gc_ref[:, at]
            k2t = k2.T
            parts = []
            for parity in range(2):
                qa, ka = pair_operands(q2, k2, length, parity)
                mine = (lanes < HEAD_DIM) if parity == 0 else (lanes >= HEAD_DIM)
                va = jnp.where(mine, v2.astype(F32), 0.0).astype(BF16)
                probs = jnp.exp(nt(ka, qa) - lse_ref[pair, parity : parity + 1, :])
                grad_v = matmul(probs.astype(BF16), g2)
                grad_probs = nt(va, g2)
                inner = jnp.sum(probs * grad_probs, 0, keepdims=True)
                grad_scores = (probs * (grad_probs - inner)).astype(BF16)
                parts.append((grad_v, matmul(grad_scores, qa), matmul(k2t, grad_scores)))
            first = lanes < HEAD_DIM
            dv_ref[:, at] = jnp.where(first, parts[0][0], parts[1][0]).astype(BF16)
            dk_ref[:, at] = jnp.where(first, parts[0][1], parts[1][1]).astype(BF16)
            turned = jnp.where(lanes_row < HEAD_DIM, parts[0][2], parts[1][2]) * HEAD_DIM ** -0.5
            dq_ref[:, at] = turned.T.astype(BF16)
            return carry

        ready = groups - 1
        for g in range(ready):
            advance(g, 0)
        lax.fori_loop(0, 1, attend, 0)
        advance(0, 1)
        advance(1, 1)
        lax.fori_loop(1, 3, attend, 0)
        advance(0, 2)
        advance(2, 1)
        lax.fori_loop(3, 5, attend, 0)
        advance(0, 3)
        advance(1, 2)
        lax.fori_loop(5, pairs, attend, 0)
        advance(0, 4)

        for j, ref in enumerate((dq_ref, dk_ref, dv_ref)):
            for h in range(2):
                value = tn(x_ref[...], ref[:, h * half : (h + 1) * half]).astype(BF16)
                shape = (2,) * (bits - 1) + (block, half)
                held[group * ready + j, h] = value.reshape(shape)
        advance(ready, 0)

        def total_of(ref):
            return jnp.sum(ref[...].astype(F32), 0, keepdims=True)

        small_buf[0] = small_in[...]
        small_buf[0, QUERY_BIAS : QUERY_BIAS + 1, :] = total_of(dq_ref)
        small_buf[0, VALUE_BIAS : VALUE_BIAS + 1, :] = total_of(dv_ref)
        side_send_stage(0)
        advance(ready, 1)
        advance(1, 3)
        advance(2, 2)
        side_add_stage(0)
        side_send_stage(1)
        grad_ref[...] = (gfirst_ref[...] + nt(dq_ref[...], wq_ref[...]) + nt(dk_ref[...], wk_ref[...])
                         + nt(dv_ref[...], wv_ref[...])).astype(BF16)
        todo = [(0, 5), (1, 4), (2, 3), (3, 2), (1, 5), (2, 4), (3, 3), (2, 5), (3, 4), (3, 5)]
        for n, (g, s) in enumerate(todo):
            advance(g, s)
            if n in (1, 3, 5, 7):
                k = 1 + n // 2
                side_add_stage(k)
                if k + 1 < stages:
                    side_send_stage(k + 1)
        for key, copy in started.items():
            for one in copy if isinstance(copy, list) else [copy]:
                one.wait_send()

    vmem = pl.BlockSpec(memory_space=pltpu.VMEM)
    anywhere = pl.BlockSpec(memory_space=pl.ANY)
    devices = 1 << bits
    pieces = [p.reshape((-1,) + grid_dims + (block, half)) for p in (up_pieces, down_pieces)]
    return pl.pallas_call(
        kernel,
        out_shape=[
            jax.ShapeDtypeStruct((rows, width), BF16), jax.ShapeDtypeStruct((count, block, half), F32),
            jax.ShapeDtypeStruct(small.shape, F32), jax.ShapeDtypeStruct((devices,) + factors.shape, factors.dtype),
        ],
        in_specs=[pl.BlockSpec(memory_space=pltpu.SMEM)] + [vmem] * 12 + [anywhere] * 3,
        out_specs=[vmem] * 4,
        scratch_shapes=[pltpu.VMEM((count,) + grid_dims + (block, half), BF16)]
        + [pltpu.VMEM((count,) + (2,) * (stages - 1 - s) + (block, half), BF16) for s in range(stages)]
        + [pltpu.VMEM((rows, width), BF16)] * 3
        + [
            pltpu.VMEM((stages,) + small.shape, F32),
            pltpu.VMEM((stages,) + small.shape, F32),
            pltpu.SemaphoreType.DMA((count - 3,)),
            pltpu.SemaphoreType.DMA((count, stages)),
            pltpu.SemaphoreType.DMA((count, stages)),
            pltpu.SemaphoreType.DMA((2, stages)),
            pltpu.SemaphoreType.DMA((2, stages)),
        ],
        compiler_params=pltpu.CompilerParams(collective_id=1, has_side_effects=True, vmem_limit_bytes=VMEM_LIMIT),
        name="attention_backward",
    )(lengths, queries, keys, values, grad_context, inputs, *full, grad_first, log_totals, small, factors,
      *pieces, out_piece.reshape(grid_dims + (block, half)))


def spread(sums, small, gathered, classes, head_size):
    count, block, half = sums.shape
    devices = gathered.shape[0]
    width = small.shape[1]
    times = (count - 4) // 2
    lanes = width // 128

    def kernel(sums_ref, small_ref, got_ref, up, down, out, query, key, value, pool, query_bias, value_bias, out_bias,
               first_gain, first_shift, up_bias, down_bias, second_gain, second_shift, pool_bias, class_weight,
               class_bias, loss, left, right):
        dp, head = lax.axis_index("dp"), lax.axis_index("head")
        for t in range(times):
            up[:, t * half : (t + 1) * half] = sums_ref[t]
            down[t * block : (t + 1) * block, :] = sums_ref[times + t]
        for k, ref in enumerate((out, query, key, value)):
            ref[...] = sums_ref[2 * times + k]
        got = got_ref[...].astype(F32)

        def wide(k):
            return jnp.concatenate([got[:, k * lanes + j, :] for j in range(lanes)], 1)

        lead, grad_pooled, pooled = wide(0), wide(1), wide(2)
        grad_logits = got[:, 3 * lanes, :]
        left[...] = lead.T
        right[...] = grad_pooled
        pool[...] = matmul(
            left[pl.ds(pl.multiple_of(dp * block, 8), block), :].astype(BF16),
            right[:, pl.ds(pl.multiple_of(head * half, half), half)].astype(BF16))
        pool_bias[...] = jnp.sum(grad_pooled, 0, keepdims=True)
        class_weight[...] = tn(pooled.astype(BF16), grad_logits.astype(BF16))[:, 0:classes]
        class_bias[...] = jnp.sum(grad_logits, 0, keepdims=True)[:, 0:classes]
        at = pl.ds(pl.multiple_of(head * half, half), half)
        query_bias[...] = small_ref[QUERY_BIAS : QUERY_BIAS + 1, at]
        value_bias[...] = small_ref[VALUE_BIAS : VALUE_BIAS + 1, at]
        for ref, row in ((out_bias, OUT_BIAS), (first_gain, FIRST_GAIN), (first_shift, FIRST_SHIFT),
                         (down_bias, DOWN_BIAS), (second_gain, SECOND_GAIN), (second_shift, SECOND_SHIFT)):
            ref[...] = small_ref[row : row + 1, :]
        for t in range(times):
            up_bias[:, t * width : (t + 1) * width] = small_ref[UP_BIAS + t : UP_BIAS + t + 1, :]
        loss[...] = small_ref[LOSS : LOSS + 1, 0:1]

    def f32(*shape):
        return jax.ShapeDtypeStruct(shape, F32)

    square = f32(block, half)
    row = f32(1, width)
    return pl.pallas_call(
        kernel,
        out_shape=[
            f32(block, times * half), f32(times * block, half), square, square, square, square, square, f32(1, half),
            f32(1, half), row, row, row, f32(1, times * width), row, row, row, row, f32(width, classes),
            f32(1, classes), f32(1, 1),
        ],
        in_specs=[pl.BlockSpec(memory_space=pltpu.VMEM)] * 3,
        out_specs=[pl.BlockSpec(memory_space=pltpu.VMEM)] * 20,
        scratch_shapes=[pltpu.VMEM((width, devices), F32), pltpu.VMEM((devices, width), F32)],
        compiler_params=pltpu.CompilerParams(vmem_limit_bytes=VMEM_LIMIT),
        name="spread",
    )(sums, small, gathered)


def plain_body(
    inputs, lengths, labels, state_cotangent, query_weight, query_bias, key_weight, value_weight, value_bias,
    out_weight, out_bias, first_gain, first_shift, up_weight, up_bias, down_weight, down_bias, second_gain,
    second_shift, pool_weight, pool_bias, class_weight, class_bias,
):
    scale = HEAD_DIM ** (-0.5)
    dp_size, head_size = lax.axis_size("dp"), lax.axis_size("head")
    dp_at, head_at = lax.axis_index("dp"), lax.axis_index("head")
    devices = dp_size * head_size
    width = inputs.shape[1]
    block_columns = width // head_size
    row_seqs = labels.shape[0]
    assert row_seqs == 1 and inputs.shape[0] == SEQ_LEN
    length = lax.dynamic_index_in_dim(lengths, head_at, keepdims=False)

    weights = [query_weight, key_weight, value_weight]
    full = [lax.all_gather(w, "head", axis=1, tiled=True) for w in weights]
    biases = lax.all_gather(jnp.stack([query_bias, value_bias]), "head", axis=1, tiled=True)
    query_bias, value_bias = biases[0], biases[1]
    wq, wk, wv = full
    head_count = width // HEAD_DIM

    def heads(matrix):
        return matrix.reshape(SEQ_LEN, head_count, HEAD_DIM)

    queries = (matmul(inputs, wq) + query_bias).astype(BF16)
    keys_low = matmul(inputs, wk).astype(BF16)
    values_low = (matmul(inputs, wv) + value_bias).astype(BF16)
    visible = lax.broadcasted_iota(jnp.int32, (1, 1, SEQ_LEN), 2) < length

    def scores_of():
        raw = jnp.einsum("qhd,khd->hqk", heads(queries), heads(keys_low), preferred_element_type=F32) * scale
        return jnp.where(visible, raw, NEGATIVE)

    scores = scores_of()
    peak = jnp.max(scores, -1, keepdims=True)
    raised = jnp.exp(scores - peak)
    denominator = jnp.sum(raised, -1, keepdims=True)
    probs = raised / denominator
    log_total = peak + jnp.log(denominator)
    context = jnp.einsum("hqk,khd->qhd", probs.astype(BF16), heads(values_low), preferred_element_type=F32)
    context_rows = context.astype(BF16).reshape(SEQ_LEN, width)
    attended = matmul(context_rows, out_weight) + out_bias
    first_out, first_back = jax.vjp(
        normalize, inputs.astype(F32) + attended, first_gain.astype(F32), first_shift.astype(F32))
    first_low = first_out.astype(BF16)
    hidden_pre = matmul(first_low, up_weight) + up_bias
    hidden_act, gelu_back = jax.vjp(partial(jax.nn.gelu, approximate=False), hidden_pre)
    hidden_low = hidden_act.astype(BF16)
    branch = matmul(hidden_low, down_weight) + down_bias
    normed, second_back = jax.vjp(normalize, first_out + branch, second_gain.astype(F32), second_shift.astype(F32))
    leading_low = normed.reshape(row_seqs, SEQ_LEN, -1)[:, 0].astype(BF16)
    pooled = jnp.tanh(matmul(leading_low, pool_weight) + pool_bias)
    pooled_low = pooled.astype(BF16)
    logits = matmul(pooled_low, class_weight) + class_bias
    classes = lax.broadcasted_iota(jnp.int32, logits.shape, 1)
    target = (classes == labels[:, None]).astype(F32)
    log_norm = jax.nn.logsumexp(logits, axis=-1)
    loss_part = jnp.sum(log_norm - jnp.sum(target * logits, -1)) / devices
    grad_logits = ((jnp.exp(logits - log_norm[:, None]) - target) / devices).astype(BF16)
    grad_class_weight = matmul(pooled_low.T, grad_logits)
    grad_class_bias = column_sums(grad_logits)
    grad_pooled = (matmul(grad_logits, class_weight.T) * (1.0 - pooled * pooled)).astype(BF16)
    grad_pool_bias = column_sums(grad_pooled)
    grad_leading = matmul(grad_pooled, pool_weight.T)
    grad_normed = state_cotangent.astype(F32).reshape(row_seqs, SEQ_LEN, -1)
    grad_normed = grad_normed.at[:, 0].add(grad_leading).reshape(normed.shape)
    grad_second, grad_second_gain, grad_second_shift = second_back(grad_normed)
    grad_branch = grad_second.astype(BF16)
    grad_down_weight = matmul(hidden_low.T, grad_branch)
    grad_down_bias = column_sums(grad_branch)
    grad_hidden = gelu_back(matmul(grad_branch, down_weight.T))[0].astype(BF16)
    grad_up_weight = matmul(first_low.T, grad_hidden)
    grad_up_bias = column_sums(grad_hidden)
    grad_first_out = grad_second + matmul(grad_hidden, up_weight.T)
    grad_first, grad_first_gain, grad_first_shift = first_back(grad_first_out)
    grad_attended = grad_first.astype(BF16)
    grad_out_weight = matmul(context_rows.T, grad_attended)
    grad_out_bias = column_sums(grad_attended)
    grad_context = heads(matmul(grad_attended, out_weight.T).astype(BF16))
    probs_again = jnp.exp(scores_of() - log_total)
    grad_values = jnp.einsum(
        "hqk,qhd->khd", probs_again.astype(BF16), grad_context, preferred_element_type=F32).astype(BF16)
    grad_probs = jnp.einsum("qhd,khd->hqk", grad_context, heads(values_low), preferred_element_type=F32)
    grad_scores = probs_again * (grad_probs - jnp.sum(probs_again * grad_probs, -1, keepdims=True))
    grad_scores = grad_scores.astype(BF16)
    grad_queries = (
        jnp.einsum("hqk,khd->qhd", grad_scores, heads(keys_low), preferred_element_type=F32) * scale).astype(BF16)
    grad_keys = (
        jnp.einsum("hqk,qhd->khd", grad_scores, heads(queries), preferred_element_type=F32) * scale).astype(BF16)
    grad_queries = grad_queries.reshape(SEQ_LEN, width)
    grad_keys = grad_keys.reshape(SEQ_LEN, width)
    grad_values = grad_values.reshape(SEQ_LEN, width)
    grad_query_weight = matmul(inputs.T, grad_queries)
    grad_key_weight = matmul(inputs.T, grad_keys)
    grad_value_weight = matmul(inputs.T, grad_values)
    input_grad = (
        grad_first + matmul(grad_queries, wq.T) + matmul(grad_keys, wk.T) + matmul(grad_values, wv.T)).astype(BF16)

    small_parts = (
        grad_out_bias, grad_first_gain, grad_first_shift, grad_up_bias, grad_down_bias, grad_second_gain,
        grad_second_shift, grad_pool_bias, column_sums(grad_queries), column_sums(grad_values),
        grad_class_weight.reshape(-1), grad_class_bias, loss_part.reshape(1),
    )
    grads = (grad_up_weight, grad_down_weight, grad_out_weight, grad_query_weight, grad_key_weight, grad_value_weight)
    grads = grads + (matmul(leading_low.T, grad_pooled),)

    def scatter(matrix):
        part = lax.psum_scatter(matrix, "dp", scatter_dimension=0, tiled=True)
        return lax.psum_scatter(part.astype(BF16), "head", scatter_dimension=1, tiled=True).astype(F32)

    up_total, down_total, out_total, query_total, key_total, value_total, pool_total = map(scatter, grads)
    totals = lax.psum(small_parts, ("dp", "head"))
    (
        out_bias_total, first_gain_total, first_shift_total, up_bias_total, down_bias_total, second_gain_total,
        second_shift_total, pool_bias_total, query_bias_total, value_bias_total, class_weight_total,
        class_bias_total, loss,
    ) = totals
    query_bias_total = lax.dynamic_slice_in_dim(query_bias_total, head_at * block_columns, block_columns)
    value_bias_total = lax.dynamic_slice_in_dim(value_bias_total, head_at * block_columns, block_columns)
    return (
        normed.astype(BF16), input_grad, logits, loss.reshape(()), query_total, query_bias_total, key_total,
        value_total, value_bias_total, out_total, out_bias_total, first_gain_total, first_shift_total, up_total,
        up_bias_total, down_total, down_bias_total, second_gain_total, second_shift_total, pool_total,
        pool_bias_total, class_weight_total.reshape(class_weight.shape), class_bias_total,
    )


def body(*args):
    (
        inputs, lengths, labels, state_cotangent, query_weight, query_bias, key_weight, value_weight, value_bias,
        out_weight, out_bias, first_gain, first_shift, up_weight, up_bias, down_weight, down_bias, second_gain,
        second_shift, pool_weight, pool_bias, class_weight, class_bias,
    ) = args
    dp_size, head_size = lax.axis_size("dp"), lax.axis_size("head")
    devices = dp_size * head_size
    bits = devices.bit_length() - 1
    rows, width = inputs.shape
    hidden = up_weight.shape[1]
    classes = class_weight.shape[1]
    times = hidden // width
    direct = (
        (width // dp_size) % 16 == 0 and head_size == 2 and bits == 5 and times == 4 and rows == SEQ_LEN
        and labels.shape[0] == 1
    )
    if not direct:
        return plain_body(*args)

    def row(vector):
        return jnp.pad(vector.astype(F32), (0, width - vector.shape[0]))

    vectors = jnp.concatenate(
        [row(v) for v in (out_bias, first_gain, first_shift, down_bias, second_gain, second_shift, pool_bias,
                          class_bias)] + [up_bias.astype(F32), jnp.zeros((4 * width,), F32)]).reshape(16, width)
    own_biases = jnp.concatenate(
        [query_bias.astype(F32), value_bias.astype(F32), jnp.zeros((6 * (width // 2),), F32)]).reshape(8, width // 2)
    class_padded = jnp.pad(class_weight, ((0, 0), (0, 128 - classes)))
    queries, keys, values, context, log_totals, *full = attention_forward(
        inputs, [query_weight, key_weight, value_weight], own_biases, lengths, bits)
    states, grad_first, grad_context, small, factors, logits, up_pieces, down_pieces, out_piece = row_side(
        context, inputs, state_cotangent, vectors, class_padded, labels, out_weight, up_weight, down_weight, pool_weight,
        devices, head_size)
    input_grad, sums, small_total, gathered = attention_backward(
        queries, keys, values, grad_context, inputs, full, grad_first, log_totals, lengths, up_pieces, down_pieces,
        out_piece, small, factors, bits)
    (
        up, down, out, query, key, value, pool, query_sum, value_sum, out_sum, first_gain_sum, first_shift_sum, up_sum,
        down_sum, second_gain_sum, second_shift_sum, pool_sum, class_sum, class_bias_sum, loss,
    ) = spread(sums, small_total, gathered, classes, head_size)

    def flat(array):
        return array.reshape(-1)

    return (
        states, input_grad, logits[0:1, 0:classes], loss.reshape(()), query, flat(query_sum), key, value,
        flat(value_sum), out, flat(out_sum), flat(first_gain_sum), flat(first_shift_sum), up, flat(up_sum), down,
        flat(down_sum), flat(second_gain_sum), flat(second_shift_sum), pool, flat(pool_sum), class_sum,
        flat(class_bias_sum),
    )


def solution(mesh):
    rows, column, both = P(("dp", "head"), None), P(None, "head"), P("dp", "head")
    one, none = P("head"), P()
    return jax.shard_map(
        body,
        mesh=mesh,
        in_specs=(rows, P("dp"), P(("dp", "head")), rows, column, one, column, column, one) + (none,) * 14,
        out_specs=(
            rows, rows, rows, none, both, one, both, both, one, both, none, none, none, both, none, both, none,
            none, none, both, none, none, none,
        ),
        check_vma=False,
    )
```

profile of v0, /device:TPU:0, one launch (start us, length us, event | category | flops | bytes accessed | tf_op | source)
XLA Modules:
  0.0 190.8 jit_solution(3627916482174690211)
XLA Ops:
  1.3 0.7 convert_element_type.35
  2.0 0.7 convert_element_type.36
  2.7 0.6 reshape.97.bias_ref
  3.3 0.7 constant_dynamic-update-slice_fusion.7
  4.0 0.7 constant_dynamic-update-slice_fusion.6
  4.7 0.7 constant_dynamic-update-slice_fusion.5
  5.4 0.7 constant_dynamic-update-slice_fusion.4
  6.0 0.7 constant_dynamic-update-slice_fusion.3
  6.7 0.7 constant_dynamic-update-slice_fusion.2
  7.4 0.7 constant_dynamic-update-slice_fusion.1
  8.1 0.7 constant_dynamic-update-slice_fusion
  8.8 0.7 convert_dynamic-update-slice_fusion
  9.5 0.6 reshape.98.vec_ref
  10.1 0.9 copy.46
  11.0 0.7 pad.13.cls_ref
  11.7 30.7 %attention_forward.1 = (bf16[512,768]{1,0:T(8,128)(2,1)}, bf16[512,768]{1,0:T(8,128)(2,1)}, bf16[512,768]{1,0:T(8,128)(2,1)}, bf16[512,768]{1,0:T(8,128)(2,1)}, ...) custom-call(s32[2]{0:T(128)} %lengths_ref.3, ...), custom_call_target="tpu_custom_call" | custom-call | tf_op jit(solution)/shard_map/attention_forward/pallas_call | solution.py:219
  42.4 44.2 %row_side.1 = (bf16[512,768]{1,0:T(8,128)(2,1)}, f32[512,768]{1,0:T(8,128)}, bf16[512,768]{1,0:T(8,128)(2,1)}, f32[16,768]{1,0:T(8,128)}, bf16[32,128]{1,0:T(8,1...) custom-call(s32[1]{0:T(128)S(6)} %copy.59.labels_ref, ...), custom_call_target="tpu_custom_call" | custom-call | tf_op jit(solution)/shard_map/row_side/pallas_call | solution.py:434
  86.6 86.0 %attention_backward.1 = (bf16[512,768]{1,0:T(8,128)(2,1)}, f32[12,48,384]{2,1,0:T(8,128)}, f32[16,768]{1,0:T(8,128)}, bf16[32,32,128]{2,1,0:T(8,128)(2,1)}) custom-call(s32[2]{0:T(128)} %lengths_ref.3, bf16[512,768]{1,0:T(8,128)(2,1)} %get-tuple-element.66.q_ref, bf16[512,768]{1,0:T(8,128)(2,1)} %get-tuple-element.67.k_ref, ...), custom_call_target="tpu_custom_call" | custom-call | tf_op jit(solution)/shard_map/attention_backward/pallas_call | solution.py:659
  172.7 0.0 copy-start
  172.7 1.3 slice.3
  173.9 2.7 %spread.1 = (f32[48,1536]{1,0:T(8,128)}, f32[192,384]{1,0:T(8,128)}, f32[48,384]{1,0:T(8,128)}, f32[48,384]{1,0:T(8,128)}, f32[48,384]{1,0:T(8,128)}, /*index=5*...) custom-call(f32[12,48,384]{2,1,0:T(8,128)} %get-tuple-element.82.sum, ...), custom_call_target="tpu_custom_call" | custom-call | tf_op jit(solution)/shard_map/spread/pallas_call | solution.py:731
  176.6 1.3 reduce
  177.9 1.3 reduce.1
  179.2 1.3 reduce.2
  180.5 1.3 reduce.3
  181.7 1.3 reduce.4
  183.0 1.3 reduce.5
  184.3 1.3 reduce.6
  185.6 1.3 reduce.7
  186.9 1.3 reduce.8
  188.2 1.7 copy.47
  189.9 0.0 copy-done
  189.9 0.9 copy.60
  (4 shorter events, 0.0 us)
Async XLA Ops:
  172.7 17.2 %copy-start = (bf16[512,768]{1,0:T(8,128)(2,1)S(1)}, bf16[512,768]{1,0:T(8,128)(2,1)}, u32[]{:S(2)}) copy-start(bf16[512,768]{1,0:T(8,128)(2,1)} %get-tuple-element.152) | copy-start | bytes 2359300
where the time goes:
time: 192 us; the launch traced here: 191 us
  Pallas kernels  164 us (85%)
  other arithmetic  19.1 us (10%)
  local copies, waits for them, and re-layouts  6.73 us (4%)
    pallas_call x1, Pallas kernels, attention_backward(): pl.pallas_call(kernel, out_shape=[jax.ShapeDtypeStruct((rows, width), BF1...  86 us
    pallas_call x1, Pallas kernels, row_side(): pl.pallas_call(kernel, out_shape=[act_low, act, act_low, jax.ShapeDtypeSt...  44.2 us
    pallas_call x1, Pallas kernels, attention_forward(): pl.pallas_call(kernel, out_shape=[act] * 4 + [jax.ShapeDtypeStruct((2 * p...  30.7 us
    pallas_call x9, other arithmetic, spread(): pl.pallas_call(kernel, out_shape=[f32(block, times * half), f32(times * b...  11.5 us
    unnamed x10, other arithmetic  6.17 us

commit v1 on v0

--- a/solution.py
+++ b/solution.py
@@ -107,8 +107,8 @@
     pairs = half // 128
     kinds = 10
 
-    def kernel(lengths_ref, x_ref, wq_ref, wk_ref, wv_ref, bias_ref, q_ref, k_ref, v_ref, ctx_ref, lse_ref, fq_ref,
-               fk_ref, fv_ref, bias_got, send, recv, bias_send, bias_recv):
+    def kernel(lengths_ref, x_ref, wq_ref, wk_ref, wv_ref, qb_ref, vb_ref, q_ref, k_ref, v_ref, ctx_ref, lse_ref,
+               fq_ref, fk_ref, fv_ref, qb_got, vb_got, send, recv, bias_send, bias_recv):
         place = Place(bits)
         head = place.head
         bit_x, bit_z = shared_rows(bits)
@@ -134,13 +134,17 @@
             copy.start()
             started[j, kind] = copy
 
-        bias_copy = pltpu.make_async_remote_copy(
-            src_ref=bias_ref, dst_ref=bias_got, send_sem=bias_send, recv_sem=bias_recv,
-            device_id=place.partner(bits - 1), device_id_type=MESH)
+        bias_copies = [
+            pltpu.make_async_remote_copy(
+                src_ref=source, dst_ref=target, send_sem=bias_send.at[n], recv_sem=bias_recv.at[n],
+                device_id=place.partner(bits - 1), device_id_type=MESH)
+            for n, (source, target) in enumerate(((qb_ref, qb_got), (vb_ref, vb_got)))
+        ]
         for j in range(3):
             mine = rows_of(x, z)
             start(j, 0, own_refs[j].at[mine, :], (mine, own), bits - 1)
-        bias_copy.start()
+        for copy in bias_copies:
+            copy.start()
 
         def forward(j, kind, where, bit):
             start(j, kind, full_refs[j].at[where], where, bit)
@@ -172,14 +176,14 @@
         def project(j, where, bias):
             value = matmul(x_ref[...], full_refs[j][:, where])
             if bias is not None:
-                value = value + bias
+                value = value + bias[...].astype(F32).reshape(1, half)
             (q_ref, k_ref, v_ref)[j][:, where] = value.astype(BF16)
 
         for j in range(3):
             full_refs[j][:, own] = own_refs[j][...]
-        project(0, own, bias_ref[0:1, :])
+        project(0, own, qb_ref)
         project(1, own, None)
-        project(2, own, bias_ref[1:2, :])
+        project(2, own, vb_ref)
 
         def attend(pair):
             attend_pair(q_ref, k_ref, v_ref, ctx_ref, lse_ref, pair, length)
@@ -196,13 +200,14 @@
         stage_two(2)
         stage_three(1)
         stage_three(2)
-        bias_copy.wait_recv()
+        for copy in bias_copies:
+            copy.wait_recv()
         stage_four(0)
-        project(0, other, bias_got[0:1, :])
+        project(0, other, qb_got)
         stage_four(1)
         project(1, other, None)
         stage_four(2)
-        project(2, other, bias_got[1:2, :])
+        project(2, other, vb_got)
 
         def late(n, carry):
             attend((1 - head) * pairs + n)
@@ -211,7 +216,8 @@
         lax.fori_loop(0, pairs, late, 0)
         for copy in started.values():
             copy.wait_send()
-        bias_copy.wait_send()
+        for copy in bias_copies:
+            copy.wait_send()
 
     vmem = pl.BlockSpec(memory_space=pltpu.VMEM)
     act = jax.ShapeDtypeStruct((rows, width), BF16)
@@ -219,13 +225,13 @@
     return pl.pallas_call(
         kernel,
         out_shape=[act] * 4 + [jax.ShapeDtypeStruct((2 * pairs, 2, rows), F32)] + [full] * 3,
-        in_specs=[pl.BlockSpec(memory_space=pltpu.SMEM)] + [vmem] * 5,
+        in_specs=[pl.BlockSpec(memory_space=pltpu.SMEM)] + [vmem] * 6,
         out_specs=[vmem] * 8,
-        scratch_shapes=[pltpu.VMEM(biases.shape, F32), pltpu.SemaphoreType.DMA((3, kinds)),
-                        pltpu.SemaphoreType.DMA((3, kinds)), pltpu.SemaphoreType.DMA, pltpu.SemaphoreType.DMA],
+        scratch_shapes=[pltpu.VMEM((half,), BF16)] * 2 + [pltpu.SemaphoreType.DMA((3, kinds))] * 2
+        + [pltpu.SemaphoreType.DMA((2,))] * 2,
         compiler_params=pltpu.CompilerParams(collective_id=0, has_side_effects=True, vmem_limit_bytes=VMEM_LIMIT),
         name="attention_forward",
-    )(lengths, inputs, *weights, biases)
+    )(lengths, inputs, *weights, *biases)
 
 
 def gelu_parts(v):
@@ -252,7 +258,7 @@
 QUERY_BIAS, VALUE_BIAS, LOSS = 6, 7, 12
 
 
-def row_side(context, inputs, cotangent, vectors, class_padded, labels, out_weight, up_weight, down_weight, pool_weight,
+def row_side(context, inputs, cotangent, vectors, class_turned, labels, out_weight, up_weight, down_weight, pool_weight,
              devices, head_size):
     rows, width = inputs.shape
     hidden = up_weight.shape[1]
@@ -262,19 +268,28 @@
     times = hidden // width
     dp_size = devices // head_size
     block = width // dp_size
-    classes_padded = class_padded.shape[1]
+    classes = class_turned.shape[0]
     per_width = width // 128
 
-    def kernel(labels_ref, ctx_ref, x_ref, vec_ref, cls_ref, ow_ref, cot_hbm, up_hbm, down_hbm, pool_hbm,
+    def kernel(labels_ref, ctx_ref, x_ref, cls_in, ow_ref, v0, v1, v2, v3, v4, v5, v6, v7, v8, cot_hbm, up_hbm, down_hbm, pool_hbm,
                states_ref, gfirst_ref, gctx_ref, small_ref, fact_ref, logit_ref, up_out, down_out, out_out,
                cot, up_w, down_w, pool_w, first, low_ref, n1, r1, n2, r2, hid, slope, acc, gb_ref, ga_ref,
-               frow, up_buf, down_buf, out_buf, load_sem, store_sem):
+               frow, vec_ref, cls_ref, up_buf, down_buf, out_buf, load_sem, store_sem):
         loads = []
         for i, (source, target) in enumerate(
             ((up_hbm, up_w), (down_hbm, down_w), (pool_hbm, pool_w), (cot_hbm, cot))):
             load = pltpu.make_async_copy(source, target, load_sem.at[i])
             load.start()
             loads.append(load)
+
+        for i, ref in enumerate((v0, v1, v2, v3, v4, v5, v6)):
+            vec_ref[i : i + 1, :] = ref[...].astype(F32).reshape(1, width)
+        vec_ref[CLASS_BIAS : CLASS_BIAS + 1, 0:classes] = v7[...].astype(F32).reshape(1, classes)
+        wide_bias = v8[...].astype(F32).reshape(1, hidden)
+        for t in range(times):
+            vec_ref[UP_BIAS + t : UP_BIAS + t + 1, :] = wide_bias[:, t * width : (t + 1) * width]
+        cls_ref[...] = jnp.zeros_like(cls_ref)
+        cls_ref[0:classes, :] = cls_in[...]
 
         def vec(i):
             return vec_ref[i : i + 1, :]
@@ -327,17 +342,17 @@
         lead = states_ref[0:16, :]
         pooled = jnp.tanh(matmul(lead, pool_w[...]) + vec(POOL_BIAS))
         pooled_low = pooled.astype(BF16)
-        logits = matmul(pooled_low, cls_ref[...]) + vec_ref[CLASS_BIAS : CLASS_BIAS + 1, 0:classes_padded]
+        logits = nt(pooled_low, cls_ref[...]) + vec_ref[CLASS_BIAS : CLASS_BIAS + 1, 0:128]
         lanes = lane_iota(logits.shape)
-        logits = jnp.where(lanes < 3, logits, NEGATIVE)
+        logits = jnp.where(lanes < classes, logits, NEGATIVE)
         top = jnp.max(logits, -1, keepdims=True)
         norm = top + jnp.log(jnp.sum(jnp.exp(logits - top), -1, keepdims=True))
         target = jnp.where(lanes == labels_ref[0], 1.0, 0.0)
-        loss = (norm - jnp.sum(jnp.where(lanes < 3, target * logits, 0.0), -1, keepdims=True)) / devices
-        grad_logits = (jnp.where(lanes < 3, jnp.exp(logits - norm) - target, 0.0) / devices).astype(BF16)
-        grad_pooled = (nt(grad_logits, cls_ref[...]) * (1.0 - pooled * pooled)).astype(BF16)
+        loss = (norm - jnp.sum(jnp.where(lanes < classes, target * logits, 0.0), -1, keepdims=True)) / devices
+        grad_logits = (jnp.where(lanes < classes, jnp.exp(logits - norm) - target, 0.0) / devices).astype(BF16)
+        grad_pooled = (matmul(grad_logits, cls_ref[...]) * (1.0 - pooled * pooled)).astype(BF16)
         grad_lead = nt(grad_pooled, pool_w[...])
-        logit_ref[...] = logits[0:8, :]
+        logit_ref[...] = logits[0:1, 0:classes]
         frow[...] = jnp.zeros_like(frow)
         for k, value in enumerate((lead, grad_pooled, pooled_low)):
             wide = value.astype(F32)
@@ -435,10 +450,10 @@
         kernel,
         out_shape=[
             act_low, act, act_low, jax.ShapeDtypeStruct((16, width), F32), jax.ShapeDtypeStruct((fact_rows, 128), BF16),
-            jax.ShapeDtypeStruct((8, classes_padded), F32), pieces, pieces,
+            jax.ShapeDtypeStruct((1, classes), F32), pieces, pieces,
             jax.ShapeDtypeStruct((2, dp_size, block, half), BF16),
         ],
-        in_specs=[pl.BlockSpec(memory_space=pltpu.SMEM)] + [vmem] * 5 + [anywhere] * 4,
+        in_specs=[pl.BlockSpec(memory_space=pltpu.SMEM)] + [vmem] * 13 + [anywhere] * 4,
         out_specs=[vmem] * 6 + [anywhere] * 3,
         scratch_shapes=[
             pltpu.VMEM((rows, width), BF16),
@@ -457,6 +472,8 @@
             pltpu.VMEM((rows, width), BF16),
             pltpu.VMEM((rows, width), BF16),
             pltpu.VMEM((fact_rows, 128), F32),
+            pltpu.VMEM((16, width), F32),
+            pltpu.VMEM((128, width), BF16),
             pltpu.VMEM((2, dp_size, block, half), BF16),
             pltpu.VMEM((2, times, 2, chunk // (times * block), block, half), BF16),
             pltpu.VMEM((2, dp_size, block, half), BF16),
@@ -465,7 +482,7 @@
         ],
         compiler_params=pltpu.CompilerParams(vmem_limit_bytes=VMEM_LIMIT),
         name="row_side",
-    )(labels, context, inputs, vectors, class_padded, out_weight, cotangent, up_weight, down_weight, pool_weight)
+    )(labels, context, inputs, class_turned, out_weight, *vectors, cotangent, up_weight, down_weight, pool_weight)
 
 
 def orders(bits):
@@ -710,33 +727,33 @@
         pool[...] = matmul(
             left[pl.ds(pl.multiple_of(dp * block, 8), block), :].astype(BF16),
             right[:, pl.ds(pl.multiple_of(head * half, half), half)].astype(BF16))
-        pool_bias[...] = jnp.sum(grad_pooled, 0, keepdims=True)
-        class_weight[...] = tn(pooled.astype(BF16), grad_logits.astype(BF16))[:, 0:classes]
-        class_bias[...] = jnp.sum(grad_logits, 0, keepdims=True)[:, 0:classes]
+        pool_bias[...] = jnp.sum(grad_pooled, 0)
+        class_weight[...] = tn(grad_logits.astype(BF16), pooled.astype(BF16))[0:classes, :]
+        class_bias[...] = jnp.sum(grad_logits, 0, keepdims=True)[:, 0:classes].reshape(classes)
         at = pl.ds(pl.multiple_of(head * half, half), half)
-        query_bias[...] = small_ref[QUERY_BIAS : QUERY_BIAS + 1, at]
-        value_bias[...] = small_ref[VALUE_BIAS : VALUE_BIAS + 1, at]
+        query_bias[...] = small_ref[QUERY_BIAS : QUERY_BIAS + 1, at].reshape(half)
+        value_bias[...] = small_ref[VALUE_BIAS : VALUE_BIAS + 1, at].reshape(half)
         for ref, row in ((out_bias, OUT_BIAS), (first_gain, FIRST_GAIN), (first_shift, FIRST_SHIFT),
                          (down_bias, DOWN_BIAS), (second_gain, SECOND_GAIN), (second_shift, SECOND_SHIFT)):
-            ref[...] = small_ref[row : row + 1, :]
-        for t in range(times):
-            up_bias[:, t * width : (t + 1) * width] = small_ref[UP_BIAS + t : UP_BIAS + t + 1, :]
-        loss[...] = small_ref[LOSS : LOSS + 1, 0:1]
+            ref[...] = small_ref[row, :]
+        up_bias[...] = jnp.concatenate(
+            [small_ref[UP_BIAS + t : UP_BIAS + t + 1, :] for t in range(times)], 1).reshape(times * width)
+        loss[()] = small_ref[LOSS, 0]
 
     def f32(*shape):
         return jax.ShapeDtypeStruct(shape, F32)
 
     square = f32(block, half)
-    row = f32(1, width)
+    row = f32(width)
     return pl.pallas_call(
         kernel,
         out_shape=[
-            f32(block, times * half), f32(times * block, half), square, square, square, square, square, f32(1, half),
-            f32(1, half), row, row, row, f32(1, times * width), row, row, row, row, f32(width, classes),
-            f32(1, classes), f32(1, 1),
+            f32(block, times * half), f32(times * block, half), square, square, square, square, square, f32(half),
+            f32(half), row, row, row, f32(times * width), row, row, row, row, f32(classes, width),
+            f32(classes), f32(),
         ],
         in_specs=[pl.BlockSpec(memory_space=pltpu.VMEM)] * 3,
-        out_specs=[pl.BlockSpec(memory_space=pltpu.VMEM)] * 20,
+        out_specs=[pl.BlockSpec(memory_space=pltpu.VMEM)] * 19 + [pl.BlockSpec(memory_space=pltpu.SMEM)],
         scratch_shapes=[pltpu.VMEM((width, devices), F32), pltpu.VMEM((devices, width), F32)],
         compiler_params=pltpu.CompilerParams(vmem_limit_bytes=VMEM_LIMIT),
         name="spread",
@@ -891,19 +908,11 @@
     if not direct:
         return plain_body(*args)
 
-    def row(vector):
-        return jnp.pad(vector.astype(F32), (0, width - vector.shape[0]))
-
-    vectors = jnp.concatenate(
-        [row(v) for v in (out_bias, first_gain, first_shift, down_bias, second_gain, second_shift, pool_bias,
-                          class_bias)] + [up_bias.astype(F32), jnp.zeros((4 * width,), F32)]).reshape(16, width)
-    own_biases = jnp.concatenate(
-        [query_bias.astype(F32), value_bias.astype(F32), jnp.zeros((6 * (width // 2),), F32)]).reshape(8, width // 2)
-    class_padded = jnp.pad(class_weight, ((0, 0), (0, 128 - classes)))
+    vectors = (out_bias, first_gain, first_shift, down_bias, second_gain, second_shift, pool_bias, class_bias, up_bias)
     queries, keys, values, context, log_totals, *full = attention_forward(
-        inputs, [query_weight, key_weight, value_weight], own_biases, lengths, bits)
+        inputs, [query_weight, key_weight, value_weight], [query_bias, value_bias], lengths, bits)
     states, grad_first, grad_context, small, factors, logits, up_pieces, down_pieces, out_piece = row_side(
-        context, inputs, state_cotangent, vectors, class_padded, labels, out_weight, up_weight, down_weight, pool_weight,
+        context, inputs, state_cotangent, vectors, class_weight.T, labels, out_weight, up_weight, down_weight, pool_weight,
         devices, head_size)
     input_grad, sums, small_total, gathered = attention_backward(
         queries, keys, values, grad_context, inputs, full, grad_first, log_totals, lengths, up_pieces, down_pieces,
@@ -913,14 +922,10 @@
         down_sum, second_gain_sum, second_shift_sum, pool_sum, class_sum, class_bias_sum, loss,
     ) = spread(sums, small_total, gathered, classes, head_size)
 
-    def flat(array):
-        return array.reshape(-1)
-
     return (
-        states, input_grad, logits[0:1, 0:classes], loss.reshape(()), query, flat(query_sum), key, value,
-        flat(value_sum), out, flat(out_sum), flat(first_gain_sum), flat(first_shift_sum), up, flat(up_sum), down,
-        flat(down_sum), flat(second_gain_sum), flat(second_shift_sum), pool, flat(pool_sum), class_sum,
-        flat(class_bias_sum),
+        states, input_grad, logits, loss, query, query_sum, key, value, value_sum, out, out_sum, first_gain_sum,
+        first_shift_sum, up, up_sum, down, down_sum, second_gain_sum, second_shift_sum, pool, pool_sum, class_sum.T,
+        class_bias_sum,
     )
 
 

time: 192 us -> 166 us (0.86)
  other arithmetic: 19.1 us -> 0 us
  local copies, waits for them, and re-layouts: 6.73 us -> 0.89 us
    pallas_call x9 -> x0, other arithmetic: 11.5 us -> none  [spread(): pl.pallas_call(kernel, out_shape=[f32(block, times * half), f32(times * b...]
    unnamed x10 -> x0, other arithmetic: 6.17 us -> none
    unnamed x5 -> x3, local copies, waits for them, and re-layouts: 3.5 us -> 0.89 us
where the time goes in v1:
time: 166 us
  Pallas kernels  163 us (98%)
    pallas_call x1, Pallas kernels, attention_backward(): pl.pallas_call(kernel, out_shape=[jax.ShapeDtypeStruct((rows, width), BF1...  86 us
    pallas_call x1, Pallas kernels, row_side(): pl.pallas_call(kernel, out_shape=[act_low, act, act_low, jax.ShapeDtypeSt...  44.1 us
    pallas_call x1, Pallas kernels, attention_forward(): pl.pallas_call(kernel, out_shape=[act] * 4 + [jax.ShapeDtypeStruct((2 * p...  30.7 us

profile of v1, /device:TPU:0, one launch (start us, length us, event | category | flops | bytes accessed | tf_op | source)
XLA Modules:
  0.0 165.7 jit_solution(10639230844201322253)
XLA Ops:
  1.3 30.7 %attention_forward.1 = (bf16[512,768]{1,0:T(8,128)(2,1)}, bf16[512,768]{1,0:T(8,128)(2,1)}, bf16[512,768]{1,0:T(8,128)(2,1)}, bf16[512,768]{1,0:T(8,128)(2,1)}, ...) custom-call(s32[2]{0:T(128)} %lengths_ref.3, ...), custom_call_target="tpu_custom_call" | custom-call | tf_op jit(solution)/shard_map/attention_forward/pallas_call | solution.py:225
  32.0 44.1 %row_side.1 = (bf16[512,768]{1,0:T(8,128)(2,1)}, f32[512,768]{1,0:T(8,128)}, bf16[512,768]{1,0:T(8,128)(2,1)}, f32[16,768]{1,0:T(8,128)}, bf16[32,128]{1,0:T(8,1...) custom-call(s32[1]{0:T(128)S(6)} %copy.47.labels_ref, ...), custom_call_target="tpu_custom_call" | custom-call | tf_op jit(solution)/shard_map/row_side/pallas_call | solution.py:449
  76.2 86.0 %attention_backward.1 = (bf16[512,768]{1,0:T(8,128)(2,1)}, f32[12,48,384]{2,1,0:T(8,128)}, f32[16,768]{1,0:T(8,128)}, bf16[32,32,128]{2,1,0:T(8,128)(2,1)}) custom-call(s32[2]{0:T(128)} %lengths_ref.3, bf16[512,768]{1,0:T(8,128)(2,1)} %get-tuple-element.66.q_ref, bf16[512,768]{1,0:T(8,128)(2,1)} %get-tuple-element.67.k_ref, ...), custom_call_target="tpu_custom_call" | custom-call | tf_op jit(solution)/shard_map/attention_backward/pallas_call | solution.py:676
  162.2 0.0 copy-start
  162.2 2.6 %spread.1 = (f32[48,1536]{1,0:T(8,128)}, f32[192,384]{1,0:T(8,128)}, f32[48,384]{1,0:T(8,128)}, f32[48,384]{1,0:T(8,128)}, f32[48,384]{1,0:T(8,128)}, /*index=5*...) custom-call(f32[12,48,384]{2,1,0:T(8,128)} %get-tuple-element.82.sum, ...), custom_call_target="tpu_custom_call" | custom-call | tf_op jit(solution)/shard_map/spread/pallas_call | solution.py:748
  164.8 0.0 copy-done
  164.8 0.9 copy.48
Async XLA Ops:
  162.2 2.6 %copy-start = (bf16[512,768]{1,0:T(8,128)(2,1)S(1)}, bf16[512,768]{1,0:T(8,128)(2,1)}, u32[]{:S(2)}) copy-start(bf16[512,768]{1,0:T(8,128)(2,1)} %get-tuple-element.129) | copy-start | bytes 2359300

commit v2 on v1

--- a/solution.py
+++ b/solution.py
@@ -14,7 +14,7 @@
 MESH = pl.DeviceIdType.MESH
 F32 = jnp.float32
 BF16 = jnp.bfloat16
-VMEM_LIMIT = 62 << 20
+VMEM_LIMIT = 67_000_000
 
 
 def normalize(values, gain, shift):
@@ -255,32 +255,128 @@
 
 
 OUT_BIAS, FIRST_GAIN, FIRST_SHIFT, DOWN_BIAS, SECOND_GAIN, SECOND_SHIFT, POOL_BIAS, CLASS_BIAS, UP_BIAS = range(9)
-QUERY_BIAS, VALUE_BIAS, LOSS = 6, 7, 12
-
-
-def row_side(context, inputs, cotangent, vectors, class_turned, labels, out_weight, up_weight, down_weight, pool_weight,
-             devices, head_size):
+LOSS = 12
+
+
+def orders(bits):
+    head = bits - 1
+    rest = list(range(2, head))
+    both = [[0, 1, head] + rest, [0, head, 1] + rest]
+    return [both + [[0] + rest[:1] + pair + rest[1:]] for pair in ([1, head], [head, 1])]
+
+
+def rest_of_layer(context, inputs, class_turned, out_weight, vectors, log_totals, cotangent, up_weight, down_weight,
+                  pool_weight, queries, keys, values, full, lengths, labels, bits):
     rows, width = inputs.shape
     hidden = up_weight.shape[1]
     half = width // 2
-    chunk = half
-    chunks = hidden // chunk
     times = hidden // width
-    dp_size = devices // head_size
-    block = width // dp_size
+    devices = 1 << bits
+    block = 2 * width // devices
     classes = class_turned.shape[0]
     per_width = width // 128
-
-    def kernel(labels_ref, ctx_ref, x_ref, cls_in, ow_ref, v0, v1, v2, v3, v4, v5, v6, v7, v8, cot_hbm, up_hbm, down_hbm, pool_hbm,
-               states_ref, gfirst_ref, gctx_ref, small_ref, fact_ref, logit_ref, up_out, down_out, out_out,
-               cot, up_w, down_w, pool_w, first, low_ref, n1, r1, n2, r2, hid, slope, acc, gb_ref, ga_ref,
-               frow, vec_ref, cls_ref, up_buf, down_buf, out_buf, load_sem, store_sem):
+    fact_rows = -(-(3 * per_width + 1) // 16) * 16
+    plans = orders(bits)
+    parts = len(plans[0])
+    lanes_part = half // parts
+    count = 2 * times + 4
+    out_at, query_at = 2 * times, 2 * times + 1
+    stages = bits
+    head = bits - 1
+    small_order = [0, 1, head] + list(range(2, head))
+    pairs = width // 128
+    dp_dims = (2,) * (bits - 1)
+
+    def kernel(lengths_ref, labels_ref, ctx_ref, x_ref, cls_in, ow_ref, v0, v1, v2, v3, v4, v5, v6, v7, v8, lse_ref,
+               cot_hbm, up_hbm, down_hbm, pool_hbm, q_hbm, k_hbm, v_hbm, wq_hbm, wk_hbm, wv_hbm,
+               states_out, grad_out, logit_ref, sums_ref, small_out, late_out, factor_out, held, *rest):
+        got = rest[:stages]
+        (gb_ref, up_w, down_w, pool_w, low_ref, n1, r1, n2, r2, hid_even, hid_odd, slope_even, slope_odd, acc, whole, frow, vec_ref, cls_ref, small_buf,
+         small_got, late_buf, late_got, load_sem, late_sem, send, recv, side_send, side_recv, whole_sem) = rest[stages:]
+        place = Place(bits)
         loads = []
         for i, (source, target) in enumerate(
-            ((up_hbm, up_w), (down_hbm, down_w), (pool_hbm, pool_w), (cot_hbm, cot))):
+            ((up_hbm, up_w), (down_hbm, down_w), (pool_hbm, pool_w), (cot_hbm, gb_ref))):
             load = pltpu.make_async_copy(source, target, load_sem.at[i])
             load.start()
             loads.append(load)
+        place.greet(range(bits))
+        length = lengths_ref[place.head]
+        slot = sum(place.mine[bit] * (1 << k) for k, bit in enumerate(small_order))
+        small_ref = small_buf.at[0]
+        hids, slopes = (hid_even, hid_odd), (slope_even, slope_odd)
+
+        def index(i, done, fixed):
+            out = [i]
+            for bit in reversed(range(bits)):
+                out.append(fixed[bit] if bit in fixed else place.mine[bit] if bit in done else slice(None))
+            return tuple(out)
+
+        def part_copy(i, s):
+            plan = plans[i // parts % 2][i % parts]
+            bit = plan[s]
+            return pltpu.make_async_remote_copy(
+                src_ref=held.at[index(i, plan[:s], {bit: 1 - place.mine[bit]})], dst_ref=got[s].at[i],
+                send_sem=send.at[i, s], recv_sem=recv.at[i, s], device_id=place.partner(bit), device_id_type=MESH)
+
+        def add_part(i, s):
+            part_copy(i, s).wait_recv()
+            where = index(i, plans[i // parts % 2][i % parts][: s + 1], {})
+            if s == stages - 1:
+                sums_ref[i] = held[where].astype(F32) + got[s][i].astype(F32)
+            else:
+                held[where] = held[where] + got[s][i]
+
+        def take(name):
+            for code in SCHEDULE[name]:
+                if code >= 2000:
+                    side_advance(code // 1000 - 2, code % 10)
+                    continue
+                i, s = code // 100 * parts + code // 10 % 10, code % 10
+                if s > 0:
+                    add_part(i, s - 1)
+                if s < stages:
+                    part_copy(i, s).start()
+
+        def take_after(step, prefix, steps):
+            for n in steps:
+                if not SCHEDULE[prefix + str(n)]:
+                    continue
+
+                @pl.when(step == n)
+                def _():
+                    take(prefix + str(n))
+
+        def put(i, wide, lead):
+            for h in range(2):
+                for m in range(parts):
+                    at = h * half + m * lanes_part
+                    held[(i * parts + m, h) + lead] = wide[..., at : at + lanes_part]
+
+        def side_copy(kind, s):
+            partner = place.partner(small_order[s])
+            if kind == 0:
+                start = (slot // (1 << s)) * (1 << s)
+                source = target = factor_out.at[pl.ds(start, 1 << s)]
+            else:
+                buf, other = ((small_buf, small_got), (late_buf, late_got))[kind - 1]
+                source, target = buf.at[s], other.at[s]
+            return pltpu.make_async_remote_copy(
+                src_ref=source, dst_ref=target, send_sem=side_send.at[kind, s], recv_sem=side_recv.at[kind, s],
+                device_id=partner, device_id_type=MESH)
+
+        def side_advance(kind, s):
+            if s > 0:
+                side_copy(kind, s - 1).wait_recv()
+                if kind > 0:
+                    buf, other, result = ((small_buf, small_got, small_out), (late_buf, late_got, late_out))[kind - 1]
+                    total = buf[s - 1] + other[s - 1]
+                    if s < stages:
+                        buf[s] = total
+                    else:
+                        result[...] = total
+            if s < stages:
+                side_copy(kind, s).start()
 
         for i, ref in enumerate((v0, v1, v2, v3, v4, v5, v6)):
             vec_ref[i : i + 1, :] = ref[...].astype(F32).reshape(1, width)
@@ -301,45 +397,68 @@
             center = value - jnp.mean(value, -1, keepdims=True)
             scale = lax.rsqrt(jnp.mean(center * center, -1, keepdims=True) + EPSILON)
             normal = center * scale
-            out = normal * vec(FIRST_GAIN) + vec(FIRST_SHIFT)
             n1[at, :] = normal
             r1[at, :] = scale
-            first[at, :] = out
-            low_ref[at, :] = out.astype(BF16)
-            acc[at, :] = jnp.zeros_like(out)
+            low_ref[at, :] = (normal * vec(FIRST_GAIN) + vec(FIRST_SHIFT)).astype(BF16)
+            acc[at, :] = jnp.zeros_like(normal)
             return carry
 
         over_rows(rows, norm_one, 0)
         loads[0].wait()
         loads[1].wait()
 
-        def forward(c, carry):
-            at = pl.ds(pl.multiple_of(c * chunk, chunk), chunk)
-            pre = matmul(low_ref[...], up_w[:, at]) + vec_ref[pl.ds(UP_BIAS + c // 2, 1), pl.ds(pl.multiple_of(lax.rem(c, 2) * half, half), half)]
-            act, deriv = gelu_parts(pre)
-            act = act.astype(BF16)
-            hid[:, at] = act
-            slope[:, at] = deriv
-            acc[...] += matmul(act, down_w[at, :])
+        def at_chunk(c):
+            return pl.ds(pl.multiple_of(c * width, width), width)
+
+        def pre_of(c, parity):
+            slopes[parity][:, at_chunk(c // 2)] = matmul(low_ref[...], up_w[:, at_chunk(c)]) + vec_ref[pl.ds(UP_BIAS + c, 1), :]
+
+        def activate(c, parity):
+            at = at_chunk(c // 2)
+            act, deriv = gelu_parts(slopes[parity][:, at])
+            hids[parity][:, at] = act.astype(BF16)
+            slopes[parity][:, at] = deriv
+
+        def add_branch(c, parity):
+            acc[...] += matmul(hids[parity][:, at_chunk(c // 2)], down_w[at_chunk(c), :])
+
+        pre_of(0, 0)
+        pre_of(1, 1)
+        activate(0, 0)
+
+        def forward(n, carry):
+            c = 2 * n
+            pre_of(c + 2, 0)
+            activate(c + 1, 1)
+            add_branch(c, 0)
+            pre_of(c + 3, 1)
+            activate(c + 2, 0)
+            add_branch(c + 1, 1)
             return carry
 
-        lax.fori_loop(0, chunks, forward, 0)
+        lax.fori_loop(0, times // 2 - 1, forward, 0)
+        activate(times - 1, 1)
+        add_branch(times - 2, 0)
+        add_branch(times - 1, 1)
 
         def norm_two(at, carry):
-            value = first[at, :] + (acc[at, :] + vec(DOWN_BIAS))
+            first = n1[at, :] * vec(FIRST_GAIN) + vec(FIRST_SHIFT)
+            value = first + (acc[at, :] + vec(DOWN_BIAS))
             center = value - jnp.mean(value, -1, keepdims=True)
             scale = lax.rsqrt(jnp.mean(center * center, -1, keepdims=True) + EPSILON)
             normal = center * scale
             n2[at, :] = normal
             r2[at, :] = scale
-            states_ref[at, :] = (normal * vec(SECOND_GAIN) + vec(SECOND_SHIFT)).astype(BF16)
+            whole[at, :] = (normal * vec(SECOND_GAIN) + vec(SECOND_SHIFT)).astype(BF16)
             return carry
 
         over_rows(rows, norm_two, 0)
+        states_copy = pltpu.make_async_copy(whole, states_out, whole_sem.at[0])
+        states_copy.start()
 
         loads[2].wait()
         loads[3].wait()
-        lead = states_ref[0:16, :]
+        lead = whole[0:16, :]
         pooled = jnp.tanh(matmul(lead, pool_w[...]) + vec(POOL_BIAS))
         pooled_low = pooled.astype(BF16)
         logits = nt(pooled_low, cls_ref[...]) + vec_ref[CLASS_BIAS : CLASS_BIAS + 1, 0:128]
@@ -359,12 +478,13 @@
             for j in range(per_width):
                 frow[k * per_width + j : k * per_width + j + 1, :] = wide[0:1, j * 128 : (j + 1) * 128]
         frow[3 * per_width : 3 * per_width + 1, :] = grad_logits.astype(F32)[0:1, 0:128]
-        fact_ref[...] = frow[...].astype(BF16)
+        factor_out[slot] = frow[...].astype(BF16)
+        take("R")
 
         def back_two(at, sums):
             gain_sum, shift_sum, bias_sum = sums
             row = at.start + lax.broadcasted_iota(jnp.int32, (ROW_BLOCK, width), 0)
-            grad = cot[at, :].astype(F32) + jnp.where(row == 0, grad_lead[0:1, :], 0.0)
+            grad = gb_ref[at, :].astype(F32) + jnp.where(row == 0, grad_lead[0:1, :], 0.0)
             normal = n2[at, :]
             e = grad * vec(SECOND_GAIN)
             value = (e - jnp.mean(e, -1, keepdims=True) - normal * jnp.mean(e * normal, -1, keepdims=True)) * r2[at, :]
@@ -376,43 +496,54 @@
 
         zero = jnp.zeros((1, width), F32)
         gain_sum, shift_sum, bias_sum = over_rows(rows, back_two, (zero, zero, zero))
-        small_ref[...] = jnp.zeros_like(small_ref)
+        small_ref[...] = jnp.zeros(small_ref.shape, F32)
         small_ref[SECOND_GAIN : SECOND_GAIN + 1, :] = gain_sum
         small_ref[SECOND_SHIFT : SECOND_SHIFT + 1, :] = shift_sum
         small_ref[DOWN_BIAS : DOWN_BIAS + 1, :] = bias_sum
         small_ref[LOSS : LOSS + 1, :] = jnp.broadcast_to(loss[0:1, 0:1], (1, width))
 
-        def stores_of(c):
-            slot = lax.rem(c, 2)
-            up = pltpu.make_async_copy(up_buf.at[slot], up_out.at[lax.rem(c, times), c // times], store_sem.at[0, slot])
-            down = pltpu.make_async_copy(
-                down_buf.at[slot], down_out.at[:, :, pl.ds(c * (chunk // (times * block)), chunk // (times * block))],
-                store_sem.at[1, slot])
-            return up, down
-
-        def backward(c, carry):
-            at = pl.ds(pl.multiple_of(c * chunk, chunk), chunk)
-            slot = lax.rem(c, 2)
-            grad = (nt(gb_ref[...], down_w[at, :]) * slope[:, at]).astype(BF16)
-            small_ref[pl.ds(UP_BIAS + c // 2, 1), pl.ds(pl.multiple_of(lax.rem(c, 2) * half, half), half)] = jnp.sum(
-                grad.astype(F32), 0, keepdims=True)
-
-            @pl.when(c >= 2)
-            def _():
-                for copy in stores_of(c - 2):
-                    copy.wait()
-
-            up_buf[slot] = tn(low_ref[...], grad).astype(BF16).reshape(dp_size, block, half)
-            wide = tn(hid[:, at], gb_ref[...]).astype(BF16).reshape(chunk // (times * block), times, block, width)
-            for t in range(times):
-                for h in range(2):
-                    down_buf[slot, t, h] = wide[:, t, :, h * half : (h + 1) * half]
-            for copy in stores_of(c):
-                copy.start()
-            acc[...] += nt(grad, up_w[:, at])
+        take("B")
+
+        def down_grads(n, carry):
+            for parity in range(2):
+                c = 2 * n + parity
+                wide = tn(hids[parity][:, at_chunk(n)], gb_ref[...]).astype(BF16).reshape(2, 2, times, block, width)
+                for t in range(times):
+                    put(t, wide[:, :, t], (lax.rem(c // 2, 2), lax.rem(c, 2)))
+                take_after(c, "D", range(parity, times, 2))
             return carry
 
-        lax.fori_loop(0, chunks, backward, 0)
+        lax.fori_loop(0, times // 2, down_grads, 0)
+
+        for parity in range(2):
+
+            def up_grads(h, carry):
+                c = 2 * h + parity
+                step = 4 * parity + 2 * h
+                grad = (nt(gb_ref[...], down_w[at_chunk(c), :]) * slopes[parity][:, at_chunk(h)]).astype(BF16)
+                small_buf[0, pl.ds(UP_BIAS + c, 1), :] = jnp.sum(grad.astype(F32), 0, keepdims=True)
+                wide = tn(low_ref[...], grad).astype(BF16)
+                for t in range(2):
+                    for m in range(parts):
+                        at = t * half + m * lanes_part
+                        held[(times + 2 * parity + t) * parts + m, h] = wide[:, at : at + lanes_part].reshape(
+                            dp_dims + (block, lanes_part))
+                take_after(step, "U", range(4 * parity, 4 * parity + 4, 2))
+                acc[...] += nt(grad, up_w[:, at_chunk(c)])
+                take_after(step + 1, "U", range(4 * parity + 1, 4 * parity + 4, 2))
+                return carry
+
+            lax.fori_loop(0, 2, up_grads, 0)
+
+        late = []
+        for i, (source, target) in enumerate((
+            (q_hbm, down_w.at[0:rows, :]), (k_hbm, down_w.at[rows : 2 * rows, :]),
+            (v_hbm, down_w.at[2 * rows : 3 * rows, :]), (wq_hbm, up_w.at[:, 0:width]),
+            (wk_hbm, up_w.at[:, width : 2 * width]), (wv_hbm, up_w.at[:, 2 * width : 3 * width]),
+        )):
+            load = pltpu.make_async_copy(source, target, late_sem.at[i])
+            load.start()
+            late.append(load)
 
         def back_one(at, sums):
             gain_sum, shift_sum, bias_sum = sums
@@ -421,8 +552,8 @@
             e = grad * vec(FIRST_GAIN)
             value = (e - jnp.mean(e, -1, keepdims=True) - normal * jnp.mean(e * normal, -1, keepdims=True)) * r1[at, :]
             rounded = value.astype(BF16)
-            gfirst_ref[at, :] = value
-            ga_ref[at, :] = rounded
+            acc[at, :] = value
+            low_ref[at, :] = rounded
             return (gain_sum + jnp.sum(grad * normal, 0, keepdims=True), shift_sum + jnp.sum(grad, 0, keepdims=True),
                     bias_sum + jnp.sum(rounded.astype(F32), 0, keepdims=True))
 
@@ -430,291 +561,196 @@
         small_ref[FIRST_GAIN : FIRST_GAIN + 1, :] = gain_sum
         small_ref[FIRST_SHIFT : FIRST_SHIFT + 1, :] = shift_sum
         small_ref[OUT_BIAS : OUT_BIAS + 1, :] = bias_sum
-        gctx_ref[...] = nt(ga_ref[...], ow_ref[...]).astype(BF16)
-        grad_out = tn(ctx_ref[...], ga_ref[...]).astype(BF16).reshape(dp_size, block, width)
-        for h in range(2):
-            out_buf[h] = grad_out[:, :, h * half : (h + 1) * half]
-        out_copy = pltpu.make_async_copy(out_buf, out_out, store_sem.at[2, 0])
-        out_copy.start()
-        for c in range(chunks - 2, chunks):
-            for copy in stores_of(c):
-                copy.wait()
-        out_copy.wait()
-
-    vmem = pl.BlockSpec(memory_space=pltpu.VMEM)
-    anywhere = pl.BlockSpec(memory_space=pl.ANY)
-    act_low, act = jax.ShapeDtypeStruct((rows, width), BF16), jax.ShapeDtypeStruct((rows, width), F32)
-    pieces = jax.ShapeDtypeStruct((times, 2, dp_size, block, half), BF16)
-    fact_rows = -(-(3 * per_width + 1) // 16) * 16
-    return pl.pallas_call(
-        kernel,
-        out_shape=[
-            act_low, act, act_low, jax.ShapeDtypeStruct((16, width), F32), jax.ShapeDtypeStruct((fact_rows, 128), BF16),
-            jax.ShapeDtypeStruct((1, classes), F32), pieces, pieces,
-            jax.ShapeDtypeStruct((2, dp_size, block, half), BF16),
-        ],
-        in_specs=[pl.BlockSpec(memory_space=pltpu.SMEM)] + [vmem] * 13 + [anywhere] * 4,
-        out_specs=[vmem] * 6 + [anywhere] * 3,
-        scratch_shapes=[
-            pltpu.VMEM((rows, width), BF16),
-            pltpu.VMEM((width, hidden), BF16),
-            pltpu.VMEM((hidden, width), BF16),
-            pltpu.VMEM((width, width), BF16),
-            pltpu.VMEM((rows, width), F32),
-            pltpu.VMEM((rows, width), BF16),
-            pltpu.VMEM((rows, width), F32),
-            pltpu.VMEM((rows, 1), F32),
-            pltpu.VMEM((rows, width), F32),
-            pltpu.VMEM((rows, 1), F32),
-            pltpu.VMEM((rows, hidden), BF16),
-            pltpu.VMEM((rows, hidden), F32),
-            pltpu.VMEM((rows, width), F32),
-            pltpu.VMEM((rows, width), BF16),
-            pltpu.VMEM((rows, width), BF16),
-            pltpu.VMEM((fact_rows, 128), F32),
-            pltpu.VMEM((16, width), F32),
-            pltpu.VMEM((128, width), BF16),
-            pltpu.VMEM((2, dp_size, block, half), BF16),
-            pltpu.VMEM((2, times, 2, chunk // (times * block), block, half), BF16),
-            pltpu.VMEM((2, dp_size, block, half), BF16),
-            pltpu.SemaphoreType.DMA((4,)),
-            pltpu.SemaphoreType.DMA((3, 2)),
-        ],
-        compiler_params=pltpu.CompilerParams(vmem_limit_bytes=VMEM_LIMIT),
-        name="row_side",
-    )(labels, context, inputs, class_turned, out_weight, *vectors, cotangent, up_weight, down_weight, pool_weight)
-
-
-def orders(bits):
-    head = bits - 1
-    rest = list(range(2, head))
-    return [[0, 1, head] + rest, [0, head, 1] + rest, [0] + rest[:1] + [1, head] + rest[1:]]
-
-
-def attention_backward(queries, keys, values, grad_context, inputs, full, grad_first, log_totals, lengths, up_pieces,
-                       down_pieces, out_piece, small, factors, bits):
-    times, _, dp_size, block, half = up_pieces.shape
-    rows, width = inputs.shape
-    plans = orders(bits)
-    group = len(plans)
-    count = 2 * times + 4
-    groups = count // group
-    grid_dims = (2,) * bits
-    stages = bits
-    head = bits - 1
-    small_order = [0, 1, head] + list(range(2, head))
-    pairs = width // 128
-
-    def kernel(lengths_ref, q_ref, k_ref, v_ref, gc_ref, x_ref, wq_ref, wk_ref, wv_ref, gfirst_ref, lse_ref, small_in,
-               factor_in, up_in, down_in, out_in, grad_ref, sums_ref, small_out, factor_out, held, *rest):
-        got = rest[:stages]
-        (dq_ref, dk_ref, dv_ref, small_buf, small_got, load_sem, send, recv, side_send, side_recv) = rest[stages:]
-        place = Place(bits)
-        loads = []
-        sources = [up_in.at[i] for i in range(times)] + [down_in.at[i] for i in range(times)] + [out_in]
-        for i, source in enumerate(sources):
-            load = pltpu.make_async_copy(source, held.at[i], load_sem.at[i])
-            load.start()
-            loads.append(load)
-        slot = sum(place.mine[bit] * (1 << k) for k, bit in enumerate(small_order))
-        factor_out[slot] = factor_in[...]
-        place.greet(range(bits))
-        length = lengths_ref[place.head]
-
-        def index(i, done, fixed, free_bits):
-            out = [i]
-            for bit in reversed(range(bits)):
-                if bit in fixed:
-                    out.append(fixed[bit])
-                elif bit in done:
-                    out.append(place.mine[bit])
-                else:
-                    out.append(free_bits[bit] if free_bits is not None else slice(None))
-            return tuple(out)
-
-        started = {}
-
-        def send_piece(i, s):
-            plan = plans[i % group]
-            bit = plan[s]
-            source = held.at[index(i, plan[:s], {bit: 1 - place.mine[bit]}, None)]
-            copy = pltpu.make_async_remote_copy(
-                src_ref=source, dst_ref=got[s].at[i], send_sem=send.at[i, s], recv_sem=recv.at[i, s],
-                device_id=place.partner(bit), device_id_type=MESH)
-            copy.start()
-            started[i, s] = copy
-
-        def add_piece(i, s):
-            started[i, s].wait_recv()
-            done = plans[i % group][: s + 1]
-            free = [bit for bit in reversed(range(bits)) if bit not in done]
-            if not free:
-                where = index(i, done, {}, None)
-                sums_ref[i] = held[where].astype(F32) + got[s][i].astype(F32)
-                return
-
-            def step(n, carry):
-                free_bits = {bit: lax.rem(n // (1 << (len(free) - 1 - k)), 2) for k, bit in enumerate(free)}
-                where = index(i, done, {}, free_bits)
-                there = (i,) + tuple(free_bits[bit] for bit in free)
-                held[where] = (held[where].astype(F32) + got[s][there].astype(F32)).astype(BF16)
-                return carry
-
-            lax.fori_loop(0, 1 << len(free), step, 0)
-
-        def advance(g, s):
-            for i in range(g * group, (g + 1) * group):
-                if s == 0:
-                    if i < len(loads):
-                        loads[i].wait()
-                else:
-                    add_piece(i, s - 1)
-                if s < stages:
-                    send_piece(i, s)
-
-        def side_send_stage(s):
-            partner = place.partner(small_order[s])
-            copies = []
-            start = (slot // (1 << s)) * (1 << s)
-            rows_at = pl.ds(start, 1 << s)
-            for k, (source, target) in enumerate(
-                ((small_buf.at[s], small_got.at[s]), (factor_out.at[rows_at], factor_out.at[rows_at]))
-            ):
-                copy = pltpu.make_async_remote_copy(
-                    src_ref=source, dst_ref=target, send_sem=side_send.at[k, s], recv_sem=side_recv.at[k, s],
-                    device_id=partner, device_id_type=MESH)
-                copy.start()
-                copies.append(copy)
-            started["side", s] = copies
-
-        def side_add_stage(s):
-            for copy in started["side", s]:
-                copy.wait_recv()
-            total = small_buf[s] + small_got[s]
-            if s < stages - 1:
-                small_buf[s + 1] = total
-            else:
-                small_out[...] = total
+        take("L0")
+        put(out_at, tn(ctx_ref[...], low_ref[...]).astype(BF16).reshape(dp_dims + (block, width)), ())
+        take("L1")
+        hids[1][:, width : 2 * width] = nt(low_ref[...], ow_ref[...]).astype(BF16)
+        take("L2")
 
         lanes_row = lax.broadcasted_iota(jnp.int32, (128, rows), 0)
-        lanes = lane_iota((rows, 128))
+        pair_lanes = lane_iota((rows, 128))
+        for load in late:
+            load.wait()
 
         def attend(pair, carry):
-            at = pl.ds(pl.multiple_of(pair * 128, 128), 128)
-            q2, k2, v2, g2 = q_ref[:, at], k_ref[:, at], v_ref[:, at], gc_ref[:, at]
+            def at(n):
+                return pl.ds(pl.multiple_of(n % 2 * width + pair * 128, 128), 128)
+
+            q2 = down_w[0:rows, at(0)]
+            k2 = down_w[rows : 2 * rows, at(0)]
+            v2 = down_w[2 * rows : 3 * rows, at(0)]
+            g2 = hids[1][:, at(3)]
             k2t = k2.T
-            parts = []
+            heads_of = []
             for parity in range(2):
                 qa, ka = pair_operands(q2, k2, length, parity)
-                mine = (lanes < HEAD_DIM) if parity == 0 else (lanes >= HEAD_DIM)
+                mine = (pair_lanes < HEAD_DIM) if parity == 0 else (pair_lanes >= HEAD_DIM)
                 va = jnp.where(mine, v2.astype(F32), 0.0).astype(BF16)
                 probs = jnp.exp(nt(ka, qa) - lse_ref[pair, parity : parity + 1, :])
                 grad_v = matmul(probs.astype(BF16), g2)
                 grad_probs = nt(va, g2)
                 inner = jnp.sum(probs * grad_probs, 0, keepdims=True)
                 grad_scores = (probs * (grad_probs - inner)).astype(BF16)
-                parts.append((grad_v, matmul(grad_scores, qa), matmul(k2t, grad_scores)))
-            first = lanes < HEAD_DIM
-            dv_ref[:, at] = jnp.where(first, parts[0][0], parts[1][0]).astype(BF16)
-            dk_ref[:, at] = jnp.where(first, parts[0][1], parts[1][1]).astype(BF16)
-            turned = jnp.where(lanes_row < HEAD_DIM, parts[0][2], parts[1][2]) * HEAD_DIM ** -0.5
-            dq_ref[:, at] = turned.T.astype(BF16)
+                heads_of.append((grad_v, matmul(grad_scores, qa), matmul(k2t, grad_scores)))
+                take_after(2 * pair + parity, "P", range(parity, 2 * pairs, 2))
+            first = pair_lanes < HEAD_DIM
+            turned = jnp.where(lanes_row < HEAD_DIM, heads_of[0][2], heads_of[1][2]) * HEAD_DIM ** -0.5
+            hids[0][:, at(0)] = turned.T.astype(BF16)
+            hids[0][:, at(1)] = jnp.where(first, heads_of[0][1], heads_of[1][1]).astype(BF16)
+            hids[1][:, at(2)] = jnp.where(first, heads_of[0][0], heads_of[1][0]).astype(BF16)
             return carry
 
-        ready = groups - 1
-        for g in range(ready):
-            advance(g, 0)
-        lax.fori_loop(0, 1, attend, 0)
-        advance(0, 1)
-        advance(1, 1)
-        lax.fori_loop(1, 3, attend, 0)
-        advance(0, 2)
-        advance(2, 1)
-        lax.fori_loop(3, 5, attend, 0)
-        advance(0, 3)
-        advance(1, 2)
-        lax.fori_loop(5, pairs, attend, 0)
-        advance(0, 4)
-
-        for j, ref in enumerate((dq_ref, dk_ref, dv_ref)):
-            for h in range(2):
-                value = tn(x_ref[...], ref[:, h * half : (h + 1) * half]).astype(BF16)
-                shape = (2,) * (bits - 1) + (block, half)
-                held[group * ready + j, h] = value.reshape(shape)
-        advance(ready, 0)
-
-        def total_of(ref):
-            return jnp.sum(ref[...].astype(F32), 0, keepdims=True)
-
-        small_buf[0] = small_in[...]
-        small_buf[0, QUERY_BIAS : QUERY_BIAS + 1, :] = total_of(dq_ref)
-        small_buf[0, VALUE_BIAS : VALUE_BIAS + 1, :] = total_of(dv_ref)
-        side_send_stage(0)
-        advance(ready, 1)
-        advance(1, 3)
-        advance(2, 2)
-        side_add_stage(0)
-        side_send_stage(1)
-        grad_ref[...] = (gfirst_ref[...] + nt(dq_ref[...], wq_ref[...]) + nt(dk_ref[...], wk_ref[...])
-                         + nt(dv_ref[...], wv_ref[...])).astype(BF16)
-        todo = [(0, 5), (1, 4), (2, 3), (3, 2), (1, 5), (2, 4), (3, 3), (2, 5), (3, 4), (3, 5)]
-        for n, (g, s) in enumerate(todo):
-            advance(g, s)
-            if n in (1, 3, 5, 7):
-                k = 1 + n // 2
-                side_add_stage(k)
-                if k + 1 < stages:
-                    side_send_stage(k + 1)
-        for key, copy in started.items():
-            for one in copy if isinstance(copy, list) else [copy]:
-                one.wait_send()
+        lax.fori_loop(0, pairs, attend, 0)
+
+        def grads_of(n):
+            return hids[n // 2][:, n % 2 * width : (n % 2 + 1) * width]
+
+        late_buf[0] = jnp.zeros(late_buf.shape[1:], F32)
+        late_buf[0, 0:1, :] = jnp.sum(grads_of(0).astype(F32), 0, keepdims=True)
+        late_buf[0, 1:2, :] = jnp.sum(grads_of(2).astype(F32), 0, keepdims=True)
+        take("Q")
+        for n in range(3):
+            put(query_at + n, tn(x_ref[...], grads_of(n)).astype(BF16).reshape(dp_dims + (block, width)), ())
+            take("W" + str(n))
+        states_copy.wait()
+        for n in range(3):
+            acc[...] += nt(grads_of(n), up_w[:, n * width : (n + 1) * width])
+            take("I" + str(n))
+        whole[...] = acc[...].astype(BF16)
+        grad_copy = pltpu.make_async_copy(whole, grad_out, whole_sem.at[1])
+        grad_copy.start()
+        for n in range(4):
+            take("T" + str(n))
+        grad_copy.wait()
+        for i in range(count * parts):
+            for s in range(stages):
+                part_copy(i, s).wait_send()
+        for s in range(stages):
+            for kind in range(3):
+                side_copy(kind, s).wait_send()
 
     vmem = pl.BlockSpec(memory_space=pltpu.VMEM)
     anywhere = pl.BlockSpec(memory_space=pl.ANY)
-    devices = 1 << bits
-    pieces = [p.reshape((-1,) + grid_dims + (block, half)) for p in (up_pieces, down_pieces)]
+    smem = pl.BlockSpec(memory_space=pltpu.SMEM)
+    act = jax.ShapeDtypeStruct((rows, width), BF16)
     return pl.pallas_call(
         kernel,
         out_shape=[
-            jax.ShapeDtypeStruct((rows, width), BF16), jax.ShapeDtypeStruct((count, block, half), F32),
-            jax.ShapeDtypeStruct(small.shape, F32), jax.ShapeDtypeStruct((devices,) + factors.shape, factors.dtype),
+            act, act, jax.ShapeDtypeStruct((1, classes), F32), jax.ShapeDtypeStruct((count * parts, block, lanes_part), F32),
+            jax.ShapeDtypeStruct((16, width), F32), jax.ShapeDtypeStruct((8, width), F32),
+            jax.ShapeDtypeStruct((devices, fact_rows, 128), BF16),
         ],
-        in_specs=[pl.BlockSpec(memory_space=pltpu.SMEM)] + [vmem] * 12 + [anywhere] * 3,
-        out_specs=[vmem] * 4,
-        scratch_shapes=[pltpu.VMEM((count,) + grid_dims + (block, half), BF16)]
-        + [pltpu.VMEM((count,) + (2,) * (stages - 1 - s) + (block, half), BF16) for s in range(stages)]
-        + [pltpu.VMEM((rows, width), BF16)] * 3
+        in_specs=[smem] * 2 + [vmem] * 14 + [anywhere] * 10,
+        out_specs=[anywhere] * 2 + [vmem] * 5,
+        scratch_shapes=[pltpu.VMEM((count * parts, 2) + dp_dims + (block, lanes_part), BF16)]
+        + [pltpu.VMEM((count * parts,) + (2,) * (stages - 1 - s) + (block, lanes_part), BF16) for s in range(stages)]
         + [
-            pltpu.VMEM((stages,) + small.shape, F32),
-            pltpu.VMEM((stages,) + small.shape, F32),
-            pltpu.SemaphoreType.DMA((count - 3,)),
-            pltpu.SemaphoreType.DMA((count, stages)),
-            pltpu.SemaphoreType.DMA((count, stages)),
-            pltpu.SemaphoreType.DMA((2, stages)),
-            pltpu.SemaphoreType.DMA((2, stages)),
+            pltpu.VMEM((rows, width), BF16),
+            pltpu.VMEM((width, hidden), BF16),
+            pltpu.VMEM((hidden, width), BF16),
+            pltpu.VMEM((width, width), BF16),
+            pltpu.VMEM((rows, width), BF16),
+            pltpu.VMEM((rows, width), F32),
+            pltpu.VMEM((rows, 1), F32),
+            pltpu.VMEM((rows, width), F32),
+            pltpu.VMEM((rows, 1), F32),
+            pltpu.VMEM((rows, hidden // 2), BF16),
+            pltpu.VMEM((rows, hidden // 2), BF16),
+            pltpu.VMEM((rows, hidden // 2), F32),
+            pltpu.VMEM((rows, hidden // 2), F32),
+            pltpu.VMEM((rows, width), F32),
+            pltpu.VMEM((rows, width), BF16),
+            pltpu.VMEM((fact_rows, 128), F32),
+            pltpu.VMEM((16, width), F32),
+            pltpu.VMEM((128, width), BF16),
+            pltpu.VMEM((stages, 16, width), F32),
+            pltpu.VMEM((stages, 16, width), F32),
+            pltpu.VMEM((stages, 8, width), F32),
+            pltpu.VMEM((stages, 8, width), F32),
+            pltpu.SemaphoreType.DMA((4,)),
+            pltpu.SemaphoreType.DMA((6,)),
+            pltpu.SemaphoreType.DMA((count * parts, stages)),
+            pltpu.SemaphoreType.DMA((count * parts, stages)),
+            pltpu.SemaphoreType.DMA((3, stages)),
+            pltpu.SemaphoreType.DMA((3, stages)),
+            pltpu.SemaphoreType.DMA((2,)),
         ],
         compiler_params=pltpu.CompilerParams(collective_id=1, has_side_effects=True, vmem_limit_bytes=VMEM_LIMIT),
-        name="attention_backward",
-    )(lengths, queries, keys, values, grad_context, inputs, *full, grad_first, log_totals, small, factors,
-      *pieces, out_piece.reshape(grid_dims + (block, half)))
-
-
-def spread(sums, small, gathered, classes, head_size):
-    count, block, half = sums.shape
+        name="rest_of_layer",
+    )(lengths, labels, context, inputs, class_turned, out_weight, *vectors, log_totals, cotangent, up_weight,
+      down_weight, pool_weight, queries, keys, values, *full)
+
+
+SCHEDULE = {
+    "R": (2000,),
+    "B": (),
+    "D0": (),
+    "D1": (2001,),
+    "D2": (),
+    "D3": (0, 10, 20, 100, 110, 120,),
+    "U0": (2002, 1, 200, 210, 220, 300, 310, 320,),
+    "U1": (11, 21, 101,),
+    "U2": (111, 121, 201, 211, 221, 400, 410, 420, 500, 510, 520,),
+    "U3": (2003, 301,),
+    "U4": (2, 12, 102,),
+    "U5": (321, 22, 122,),
+    "U6": (112, 202, 212, 311, 421, 600, 610, 620, 700, 710, 720,),
+    "U7": (222,),
+    "L0": (3000, 3, 13, 103, 302, 401,),
+    "L1": (2004, 23, 322, 521, 800, 810, 820,),
+    "L2": (123, 411, 501,),
+    "P0": (3001, 113, 203,),
+    "P1": (4, 14, 213, 223, 104, 621,),
+    "P2": (24, 312, 511,),
+    "P3": (124, 303, 323, 721,),
+    "P4": (114, 204, 402, 422,),
+    "P5": (214, 412, 224, 5, 502, 522, 601, 821,),
+    "P6": (2005, 15, 25, 105, 611,),
+    "P7": (3002, 115, 125, 304, 313, 324, 512, 205,),
+    "P8": (215, 403, 622,),
+    "P9": (225, 413, 423, 503, 701,),
+    "P10": (711,),
+    "P11": (305, 325, 523, 314,),
+    "Q": (4000, 602, 801,),
+    "W0": (404, 414, 513, 722, 900, 910, 920,),
+    "W1": (424, 504, 612, 623, 1000, 1010, 1020,),
+    "W2": (3003, 315, 811, 822, 1100, 4001, 1110, 1120,),
+    "I0": (405, 514, 524, 921,),
+    "I1": (415, 425, 603, 702, 712, 1021,),
+    "I2": (505, 723, 802, 624, 901, 911,),
+    "T0": (1001, 1011, 1101, 1111, 1121, 613, 515, 3004, 525, 823, 922, 812, 604, 713, 703, 625, 4002, 724, 803,),
+    "T1": (1022, 605, 902, 912, 725, 3005, 1122, 614, 714, 1002, 704, 1012, 804, 1102, 615, 1112, 715, 813, 824,),
+    "T2": (705, 805, 1023, 923, 913, 814, 903, 825, 4003, 1013, 1123, 1113, 914, 924, 1003, 904, 815, 1103, 1014,),
+    "T3": (1124, 1024, 1114, 4004, 1004, 915, 925, 1104, 905, 1015, 1125, 1025, 1115, 1005, 1105, 4005,),
+}
+
+
+def spread(states, input_grad, logits, sums, small, late, gathered, classes):
+    width = small.shape[1]
+    half = width // 2
+    parts, block, lanes_part = sums.shape
+    count = parts * lanes_part // half
+    parts = parts // count
     devices = gathered.shape[0]
-    width = small.shape[1]
     times = (count - 4) // 2
     lanes = width // 128
 
-    def kernel(sums_ref, small_ref, got_ref, up, down, out, query, key, value, pool, query_bias, value_bias, out_bias,
-               first_gain, first_shift, up_bias, down_bias, second_gain, second_shift, pool_bias, class_weight,
-               class_bias, loss, left, right):
+    def kernel(states_ref, grad_ref, logits_ref, sums_ref, small_ref, late_ref, got_ref, states_out, grad_out, logits_out, up, down,
+               out, query, key, value, pool, query_bias, value_bias, out_bias, first_gain, first_shift, up_bias,
+               down_bias, second_gain, second_shift, pool_bias, class_weight, class_bias, loss, left, right, sem):
+        copies = [
+            pltpu.make_async_copy(states_ref, states_out, sem.at[0]), pltpu.make_async_copy(grad_ref, grad_out, sem.at[1])]
+        for copy in copies:
+            copy.start()
+        logits_out[...] = logits_ref[...]
         dp, head = lax.axis_index("dp"), lax.axis_index("head")
-        for t in range(times):
-            up[:, t * half : (t + 1) * half] = sums_ref[t]
-            down[t * block : (t + 1) * block, :] = sums_ref[times + t]
-        for k, ref in enumerate((out, query, key, value)):
-            ref[...] = sums_ref[2 * times + k]
+        for m in range(parts):
+            at = slice(m * lanes_part, (m + 1) * lanes_part)
+            for t in range(times):
+                down[t * block : (t + 1) * block, at] = sums_ref[t * parts + m]
+                up[:, t * half + m * lanes_part : t * half + (m + 1) * lanes_part] = sums_ref[(times + t) * parts + m]
+            for k, ref in enumerate((out, query, key, value)):
+                ref[:, at] = sums_ref[(2 * times + k) * parts + m]
         got = got_ref[...].astype(F32)
 
         def wide(k):
@@ -724,40 +760,45 @@
         grad_logits = got[:, 3 * lanes, :]
         left[...] = lead.T
         right[...] = grad_pooled
+        at = pl.ds(pl.multiple_of(head * half, half), half)
         pool[...] = matmul(
-            left[pl.ds(pl.multiple_of(dp * block, 8), block), :].astype(BF16),
-            right[:, pl.ds(pl.multiple_of(head * half, half), half)].astype(BF16))
+            left[pl.ds(pl.multiple_of(dp * block, 8), block), :].astype(BF16), right[:, at].astype(BF16))
         pool_bias[...] = jnp.sum(grad_pooled, 0)
         class_weight[...] = tn(grad_logits.astype(BF16), pooled.astype(BF16))[0:classes, :]
         class_bias[...] = jnp.sum(grad_logits, 0, keepdims=True)[:, 0:classes].reshape(classes)
-        at = pl.ds(pl.multiple_of(head * half, half), half)
-        query_bias[...] = small_ref[QUERY_BIAS : QUERY_BIAS + 1, at].reshape(half)
-        value_bias[...] = small_ref[VALUE_BIAS : VALUE_BIAS + 1, at].reshape(half)
+        query_bias[...] = late_ref[0:1, at].reshape(half)
+        value_bias[...] = late_ref[1:2, at].reshape(half)
         for ref, row in ((out_bias, OUT_BIAS), (first_gain, FIRST_GAIN), (first_shift, FIRST_SHIFT),
                          (down_bias, DOWN_BIAS), (second_gain, SECOND_GAIN), (second_shift, SECOND_SHIFT)):
             ref[...] = small_ref[row, :]
         up_bias[...] = jnp.concatenate(
             [small_ref[UP_BIAS + t : UP_BIAS + t + 1, :] for t in range(times)], 1).reshape(times * width)
         loss[()] = small_ref[LOSS, 0]
+        for copy in copies:
+            copy.wait()
 
     def f32(*shape):
         return jax.ShapeDtypeStruct(shape, F32)
 
     square = f32(block, half)
     row = f32(width)
+    act = jax.ShapeDtypeStruct(states.shape, BF16)
+    vmem = pl.BlockSpec(memory_space=pltpu.VMEM)
+    anywhere = pl.BlockSpec(memory_space=pl.ANY)
     return pl.pallas_call(
         kernel,
         out_shape=[
-            f32(block, times * half), f32(times * block, half), square, square, square, square, square, f32(half),
-            f32(half), row, row, row, f32(times * width), row, row, row, row, f32(classes, width),
+            act, act, f32(1, classes), f32(block, times * half), f32(times * block, half), square, square, square, square,
+            square, f32(half), f32(half), row, row, row, f32(times * width), row, row, row, row, f32(classes, width),
             f32(classes), f32(),
         ],
-        in_specs=[pl.BlockSpec(memory_space=pltpu.VMEM)] * 3,
-        out_specs=[pl.BlockSpec(memory_space=pltpu.VMEM)] * 19 + [pl.BlockSpec(memory_space=pltpu.SMEM)],
-        scratch_shapes=[pltpu.VMEM((width, devices), F32), pltpu.VMEM((devices, width), F32)],
+        in_specs=[vmem] * 7,
+        out_specs=[anywhere] * 2 + [vmem] * 20 + [pl.BlockSpec(memory_space=pltpu.SMEM)],
+        scratch_shapes=[
+            pltpu.VMEM((width, devices), F32), pltpu.VMEM((devices, width), F32), pltpu.SemaphoreType.DMA((2,))],
         compiler_params=pltpu.CompilerParams(vmem_limit_bytes=VMEM_LIMIT),
         name="spread",
-    )(sums, small, gathered)
+    )(states, input_grad, logits, sums, small, late, gathered)
 
 
 def plain_body(
@@ -900,28 +941,23 @@
     rows, width = inputs.shape
     hidden = up_weight.shape[1]
     classes = class_weight.shape[1]
-    times = hidden // width
     direct = (
-        (width // dp_size) % 16 == 0 and head_size == 2 and bits == 5 and times == 4 and rows == SEQ_LEN
+        (width // dp_size) % 16 == 0 and head_size == 2 and bits == 5 and hidden == 4 * width and rows == SEQ_LEN
         and labels.shape[0] == 1
     )
     if not direct:
         return plain_body(*args)
 
-    vectors = (out_bias, first_gain, first_shift, down_bias, second_gain, second_shift, pool_bias, class_bias, up_bias)
     queries, keys, values, context, log_totals, *full = attention_forward(
         inputs, [query_weight, key_weight, value_weight], [query_bias, value_bias], lengths, bits)
-    states, grad_first, grad_context, small, factors, logits, up_pieces, down_pieces, out_piece = row_side(
-        context, inputs, state_cotangent, vectors, class_weight.T, labels, out_weight, up_weight, down_weight, pool_weight,
-        devices, head_size)
-    input_grad, sums, small_total, gathered = attention_backward(
-        queries, keys, values, grad_context, inputs, full, grad_first, log_totals, lengths, up_pieces, down_pieces,
-        out_piece, small, factors, bits)
+    vectors = (out_bias, first_gain, first_shift, down_bias, second_gain, second_shift, pool_bias, class_bias, up_bias)
+    states, input_grad, logits, sums, small, late, gathered = rest_of_layer(
+        context, inputs, class_weight.T, out_weight, vectors, log_totals, state_cotangent, up_weight, down_weight,
+        pool_weight, queries, keys, values, full, lengths, labels, bits)
     (
-        up, down, out, query, key, value, pool, query_sum, value_sum, out_sum, first_gain_sum, first_shift_sum, up_sum,
-        down_sum, second_gain_sum, second_shift_sum, pool_sum, class_sum, class_bias_sum, loss,
-    ) = spread(sums, small_total, gathered, classes, head_size)
-
+        states, input_grad, logits, up, down, out, query, key, value, pool, query_sum, value_sum, out_sum, first_gain_sum,
+        first_shift_sum, up_sum, down_sum, second_gain_sum, second_shift_sum, pool_sum, class_sum, class_bias_sum, loss,
+    ) = spread(states, input_grad, logits, sums, small, late, gathered, classes)
     return (
         states, input_grad, logits, loss, query, query_sum, key, value, value_sum, out, out_sum, first_gain_sum,
         first_shift_sum, up, up_sum, down, down_sum, second_gain_sum, second_shift_sum, pool, pool_sum, class_sum.T,

time: 166 us -> 137 us (0.83)
  Pallas kernels: 163 us -> 135 us
    pallas_call x3 -> x2, Pallas kernels: 133 us -> 104 us  [the longest x1 100 us: rest_of_layer(): pl.pallas_call(kernel, out_shape=[act, act, jax.ShapeDtypeStruct((1, clas...]
where the time goes in v2:
time: 137 us; the launch traced here: 136 us
  Pallas kernels  135 us (99%)
  between operations  1.52 us (1%)
    pallas_call x1, Pallas kernels, rest_of_layer(): pl.pallas_call(kernel, out_shape=[act, act, jax.ShapeDtypeStruct((1, clas...  100 us
    pallas_call x1, Pallas kernels, attention_forward(): pl.pallas_call(kernel, out_shape=[act] * 4 + [jax.ShapeDtypeStruct((2 * p...  30.6 us
    pallas_call x1, Pallas kernels, spread(): pl.pallas_call(kernel, out_shape=[act, act, f32(1, classes), f32(block, t...  3.9 us

profile of v2, /device:TPU:0, one launch (start us, length us, event | category | flops | bytes accessed | tf_op | source)
XLA Modules:
  0.0 136.5 jit_solution(8589475995026649837)
XLA Ops:
  1.3 30.6 %attention_forward.1 = (bf16[512,768]{1,0:T(8,128)(2,1)}, bf16[512,768]{1,0:T(8,128)(2,1)}, bf16[512,768]{1,0:T(8,128)(2,1)}, bf16[512,768]{1,0:T(8,128)(2,1)}, ...) custom-call(s32[2]{0:T(128)} %lengths_ref.3, ...), custom_call_target="tpu_custom_call" | custom-call | tf_op jit(solution)/shard_map/attention_forward/pallas_call | solution.py:225
  31.9 100.4 %rest_of_layer.1 = (bf16[512,768]{1,0:T(8,128)(2,1)}, bf16[512,768]{1,0:T(8,128)(2,1)}, f32[1,3]{1,0:T(1,128)}, f32[36,48,128]{2,1,0:T(8,128)}, f32[16,768]{1,0:...) custom-call(s32[2]{0:T(128)} %lengths_ref.3, s32[1]{0:T(128)S(6)} %copy.46.labels_ref, ...), custom_call_target="tpu_custom_call" | custom-call | tf_op jit(solution)/shard_map/rest_of_layer/pallas_call | solution.py:636
  132.4 3.9 %spread.1 = (bf16[512,768]{1,0:T(8,128)(2,1)}, bf16[512,768]{1,0:T(8,128)(2,1)}, f32[1,3]{1,0:T(1,128)}, f32[48,1536]{1,0:T(8,128)}, f32[192,384]{1,0:T(8,128)},...) custom-call(bf16[512,768]{1,0:T(8,128)(2,1)} %get-tuple-element.69.s, ...), custom_call_target="tpu_custom_call" | custom-call | tf_op jit(solution)/shard_map/spread/pallas_call | solution.py:788

commit v3 on v2

--- a/solution.py
+++ b/solution.py
@@ -107,8 +107,9 @@
     pairs = half // 128
     kinds = 10
 
-    def kernel(lengths_ref, x_ref, wq_ref, wk_ref, wv_ref, qb_ref, vb_ref, q_ref, k_ref, v_ref, ctx_ref, lse_ref,
-               fq_ref, fk_ref, fv_ref, qb_got, vb_got, send, recv, bias_send, bias_recv):
+    def kernel(lengths_ref, x_ref, wq_ref, wk_ref, wv_ref, qb_ref, vb_ref, q_out, k_out, v_out, ctx_ref, lse_ref,
+               fq_out, fk_out, fv_out, q_ref, k_ref, v_ref, fq_ref, fk_ref, fv_ref, qb_got, vb_got, send, recv,
+               bias_send, bias_recv, out_sem):
         place = Place(bits)
         head = place.head
         bit_x, bit_z = shared_rows(bits)
@@ -209,16 +210,26 @@
         stage_four(2)
         project(2, other, vb_got)
 
+        outs = []
+        for n, (source, target) in enumerate((
+            (q_ref, q_out), (k_ref, k_out), (v_ref, v_out), (fq_ref, fq_out), (fk_ref, fk_out), (fv_ref, fv_out))):
+            copy = pltpu.make_async_copy(source, target, out_sem.at[n])
+            copy.start()
+            outs.append(copy)
+
         def late(n, carry):
             attend((1 - head) * pairs + n)
             return carry
 
         lax.fori_loop(0, pairs, late, 0)
+        for copy in outs:
+            copy.wait()
         for copy in started.values():
             copy.wait_send()
         for copy in bias_copies:
             copy.wait_send()
 
+    anywhere = pl.BlockSpec(memory_space=pl.ANY)
     vmem = pl.BlockSpec(memory_space=pltpu.VMEM)
     act = jax.ShapeDtypeStruct((rows, width), BF16)
     full = jax.ShapeDtypeStruct((depth, width), BF16)
@@ -226,9 +237,10 @@
         kernel,
         out_shape=[act] * 4 + [jax.ShapeDtypeStruct((2 * pairs, 2, rows), F32)] + [full] * 3,
         in_specs=[pl.BlockSpec(memory_space=pltpu.SMEM)] + [vmem] * 6,
-        out_specs=[vmem] * 8,
-        scratch_shapes=[pltpu.VMEM((half,), BF16)] * 2 + [pltpu.SemaphoreType.DMA((3, kinds))] * 2
-        + [pltpu.SemaphoreType.DMA((2,))] * 2,
+        out_specs=[anywhere] * 3 + [vmem] * 2 + [anywhere] * 3,
+        scratch_shapes=[pltpu.VMEM((rows, width), BF16)] * 3 + [pltpu.VMEM((depth, width), BF16)] * 3
+        + [pltpu.VMEM((half,), BF16)] * 2 + [pltpu.SemaphoreType.DMA((3, kinds))] * 2
+        + [pltpu.SemaphoreType.DMA((2,))] * 2 + [pltpu.SemaphoreType.DMA((6,))],
         compiler_params=pltpu.CompilerParams(collective_id=0, has_side_effects=True, vmem_limit_bytes=VMEM_LIMIT),
         name="attention_forward",
     )(lengths, inputs, *weights, *biases)
@@ -256,6 +268,7 @@
 
 OUT_BIAS, FIRST_GAIN, FIRST_SHIFT, DOWN_BIAS, SECOND_GAIN, SECOND_SHIFT, POOL_BIAS, CLASS_BIAS, UP_BIAS = range(9)
 LOSS = 12
+CLASS_ROWS = (6, 7, 13)
 
 
 def orders(bits):
@@ -275,7 +288,9 @@
     block = 2 * width // devices
     classes = class_turned.shape[0]
     per_width = width // 128
-    fact_rows = -(-(3 * per_width + 1) // 16) * 16
+    fact_rows = -(-2 * per_width // 16) * 16
+    small_half = 8
+    late_lanes = width // 3
     plans = orders(bits)
     parts = len(plans[0])
     lanes_part = half // parts
@@ -283,7 +298,7 @@
     out_at, query_at = 2 * times, 2 * times + 1
     stages = bits
     head = bits - 1
-    small_order = [0, 1, head] + list(range(2, head))
+    small_order = [1, head] + list(range(2, head)) + [0]
     pairs = width // 128
     dp_dims = (2,) * (bits - 1)
 
@@ -291,8 +306,8 @@
                cot_hbm, up_hbm, down_hbm, pool_hbm, q_hbm, k_hbm, v_hbm, wq_hbm, wk_hbm, wv_hbm,
                states_out, grad_out, logit_ref, sums_ref, small_out, late_out, factor_out, held, *rest):
         got = rest[:stages]
-        (gb_ref, up_w, down_w, pool_w, low_ref, n1, r1, n2, r2, hid_even, hid_odd, slope_even, slope_odd, acc, whole, frow, vec_ref, cls_ref, small_buf,
-         small_got, late_buf, late_got, load_sem, late_sem, send, recv, side_send, side_recv, whole_sem) = rest[stages:]
+        (gb_ref, up_w, down_w, pool_w, low_ref, n1, r1, n2, r2, hid_even, hid_odd, slope_even, slope_odd, acc, whole, frow, vec_ref, cls_ref, small_ref,
+         small_buf, small_got, late_buf, late_got, load_sem, late_sem, send, recv, side_send, side_recv, whole_sem) = rest[stages:]
         place = Place(bits)
         loads = []
         for i, (source, target) in enumerate(
@@ -303,7 +318,6 @@
         place.greet(range(bits))
         length = lengths_ref[place.head]
         slot = sum(place.mine[bit] * (1 << k) for k, bit in enumerate(small_order))
-        small_ref = small_buf.at[0]
         hids, slopes = (hid_even, hid_odd), (slope_even, slope_odd)
 
         def index(i, done, fixed):
@@ -354,28 +368,45 @@
                     held[(i * parts + m, h) + lead] = wide[..., at : at + lanes_part]
 
         def side_copy(kind, s):
-            partner = place.partner(small_order[s])
+            bit = small_order[s % stages]
             if kind == 0:
                 start = (slot // (1 << s)) * (1 << s)
                 source = target = factor_out.at[pl.ds(start, 1 << s)]
+            elif kind == 2:
+                source, target = late_buf.at[s], late_got.at[s]
             else:
-                buf, other = ((small_buf, small_got), (late_buf, late_got))[kind - 1]
-                source, target = buf.at[s], other.at[s]
+                bit = small_order[(s - 1) % stages]
+                if s == 0:
+                    source, target = small_ref.at[rows_of_core(1 - place.mine[0])], small_got.at[0]
+                elif s == stages:
+                    source = target = small_out.at[rows_of_core(place.mine[0])]
+                else:
+                    source, target = small_buf.at[s], small_got.at[s]
             return pltpu.make_async_remote_copy(
                 src_ref=source, dst_ref=target, send_sem=side_send.at[kind, s], recv_sem=side_recv.at[kind, s],
-                device_id=partner, device_id_type=MESH)
+                device_id=place.partner(bit), device_id_type=MESH)
+
+        def rows_of_core(core):
+            return pl.ds(pl.multiple_of(core * small_half, small_half), small_half)
 
         def side_advance(kind, s):
+            last = stages + (kind == 1)
             if s > 0:
                 side_copy(kind, s - 1).wait_recv()
-                if kind > 0:
-                    buf, other, result = ((small_buf, small_got, small_out), (late_buf, late_got, late_out))[kind - 1]
-                    total = buf[s - 1] + other[s - 1]
-                    if s < stages:
-                        buf[s] = total
-                    else:
-                        result[...] = total
-            if s < stages:
+            if kind == 1 and 0 < s < last:
+                mine = rows_of_core(place.mine[0])
+                total = (small_ref[mine, :] if s == 1 else small_buf[s - 1]) + small_got[s - 1]
+                if s < stages:
+                    small_buf[s] = total
+                else:
+                    small_out[mine, :] = total
+            if kind == 2 and s > 0:
+                total = late_buf[s - 1] + late_got[s - 1]
+                if s < stages:
+                    late_buf[s] = total
+                else:
+                    late_out[...] = total
+            if s < last:
                 side_copy(kind, s).start()
 
         for i, ref in enumerate((v0, v1, v2, v3, v4, v5, v6)):
@@ -473,11 +504,15 @@
         grad_lead = nt(grad_pooled, pool_w[...])
         logit_ref[...] = logits[0:1, 0:classes]
         frow[...] = jnp.zeros_like(frow)
-        for k, value in enumerate((lead, grad_pooled, pooled_low)):
+        for k, value in enumerate((lead, grad_pooled)):
             wide = value.astype(F32)
             for j in range(per_width):
                 frow[k * per_width + j : k * per_width + j + 1, :] = wide[0:1, j * 128 : (j + 1) * 128]
-        frow[3 * per_width : 3 * per_width + 1, :] = grad_logits.astype(F32)[0:1, 0:128]
+        small_ref[...] = jnp.zeros(small_ref.shape, F32)
+        logit_row = grad_logits.astype(F32)[0:1, :]
+        pooled_row = pooled_low.astype(F32)[0:1, :]
+        for k in range(classes):
+            small_ref[CLASS_ROWS[k] : CLASS_ROWS[k] + 1, :] = logit_row[:, k : k + 1] * pooled_row
         factor_out[slot] = frow[...].astype(BF16)
         take("R")
 
@@ -496,11 +531,11 @@
 
         zero = jnp.zeros((1, width), F32)
         gain_sum, shift_sum, bias_sum = over_rows(rows, back_two, (zero, zero, zero))
-        small_ref[...] = jnp.zeros(small_ref.shape, F32)
         small_ref[SECOND_GAIN : SECOND_GAIN + 1, :] = gain_sum
         small_ref[SECOND_SHIFT : SECOND_SHIFT + 1, :] = shift_sum
         small_ref[DOWN_BIAS : DOWN_BIAS + 1, :] = bias_sum
-        small_ref[LOSS : LOSS + 1, :] = jnp.broadcast_to(loss[0:1, 0:1], (1, width))
+        small_ref[LOSS : LOSS + 1, 0:128] = jnp.broadcast_to(loss[0:1, 0:1], (1, 128))
+        small_ref[LOSS : LOSS + 1, 128:256] = logit_row
 
         take("B")
 
@@ -521,7 +556,7 @@
                 c = 2 * h + parity
                 step = 4 * parity + 2 * h
                 grad = (nt(gb_ref[...], down_w[at_chunk(c), :]) * slopes[parity][:, at_chunk(h)]).astype(BF16)
-                small_buf[0, pl.ds(UP_BIAS + c, 1), :] = jnp.sum(grad.astype(F32), 0, keepdims=True)
+                small_ref[pl.ds(UP_BIAS + c, 1), :] = jnp.sum(grad.astype(F32), 0, keepdims=True)
                 wide = tn(low_ref[...], grad).astype(BF16)
                 for t in range(2):
                     for m in range(parts):
@@ -606,8 +641,10 @@
             return hids[n // 2][:, n % 2 * width : (n % 2 + 1) * width]
 
         late_buf[0] = jnp.zeros(late_buf.shape[1:], F32)
-        late_buf[0, 0:1, :] = jnp.sum(grads_of(0).astype(F32), 0, keepdims=True)
-        late_buf[0, 1:2, :] = jnp.sum(grads_of(2).astype(F32), 0, keepdims=True)
+        for n in range(2):
+            total = jnp.sum(grads_of(2 * n).astype(F32), 0, keepdims=True)
+            for t in range(3):
+                late_buf[0, 3 * n + t : 3 * n + t + 1, :] = total[:, t * late_lanes : (t + 1) * late_lanes]
         take("Q")
         for n in range(3):
             put(query_at + n, tn(x_ref[...], grads_of(n)).astype(BF16).reshape(dp_dims + (block, width)), ())
@@ -628,6 +665,7 @@
         for s in range(stages):
             for kind in range(3):
                 side_copy(kind, s).wait_send()
+        side_copy(1, stages).wait_send()
 
     vmem = pl.BlockSpec(memory_space=pltpu.VMEM)
     anywhere = pl.BlockSpec(memory_space=pl.ANY)
@@ -637,7 +675,7 @@
         kernel,
         out_shape=[
             act, act, jax.ShapeDtypeStruct((1, classes), F32), jax.ShapeDtypeStruct((count * parts, block, lanes_part), F32),
-            jax.ShapeDtypeStruct((16, width), F32), jax.ShapeDtypeStruct((8, width), F32),
+            jax.ShapeDtypeStruct((16, width), F32), jax.ShapeDtypeStruct((8, late_lanes), F32),
             jax.ShapeDtypeStruct((devices, fact_rows, 128), BF16),
         ],
         in_specs=[smem] * 2 + [vmem] * 14 + [anywhere] * 10,
@@ -663,16 +701,17 @@
             pltpu.VMEM((fact_rows, 128), F32),
             pltpu.VMEM((16, width), F32),
             pltpu.VMEM((128, width), BF16),
-            pltpu.VMEM((stages, 16, width), F32),
-            pltpu.VMEM((stages, 16, width), F32),
-            pltpu.VMEM((stages, 8, width), F32),
-            pltpu.VMEM((stages, 8, width), F32),
+            pltpu.VMEM((16, width), F32),
+            pltpu.VMEM((stages, small_half, width), F32),
+            pltpu.VMEM((stages, small_half, width), F32),
+            pltpu.VMEM((stages, 8, late_lanes), F32),
+            pltpu.VMEM((stages, 8, late_lanes), F32),
             pltpu.SemaphoreType.DMA((4,)),
             pltpu.SemaphoreType.DMA((6,)),
             pltpu.SemaphoreType.DMA((count * parts, stages)),
             pltpu.SemaphoreType.DMA((count * parts, stages)),
-            pltpu.SemaphoreType.DMA((3, stages)),
-            pltpu.SemaphoreType.DMA((3, stages)),
+            pltpu.SemaphoreType.DMA((3, stages + 1)),
+            pltpu.SemaphoreType.DMA((3, stages + 1)),
             pltpu.SemaphoreType.DMA((2,)),
         ],
         compiler_params=pltpu.CompilerParams(collective_id=1, has_side_effects=True, vmem_limit_bytes=VMEM_LIMIT),
@@ -682,46 +721,50 @@
 
 
 SCHEDULE = {
-    "R": (2000,),
+    "R": (),
     "B": (),
     "D0": (),
-    "D1": (2001,),
+    "D1": (),
     "D2": (),
     "D3": (0, 10, 20, 100, 110, 120,),
-    "U0": (2002, 1, 200, 210, 220, 300, 310, 320,),
-    "U1": (11, 21, 101,),
-    "U2": (111, 121, 201, 211, 221, 400, 410, 420, 500, 510, 520,),
-    "U3": (2003, 301,),
-    "U4": (2, 12, 102,),
-    "U5": (321, 22, 122,),
-    "U6": (112, 202, 212, 311, 421, 600, 610, 620, 700, 710, 720,),
-    "U7": (222,),
-    "L0": (3000, 3, 13, 103, 302, 401,),
-    "L1": (2004, 23, 322, 521, 800, 810, 820,),
-    "L2": (123, 411, 501,),
-    "P0": (3001, 113, 203,),
-    "P1": (4, 14, 213, 223, 104, 621,),
-    "P2": (24, 312, 511,),
-    "P3": (124, 303, 323, 721,),
-    "P4": (114, 204, 402, 422,),
-    "P5": (214, 412, 224, 5, 502, 522, 601, 821,),
-    "P6": (2005, 15, 25, 105, 611,),
-    "P7": (3002, 115, 125, 304, 313, 324, 512, 205,),
-    "P8": (215, 403, 622,),
-    "P9": (225, 413, 423, 503, 701,),
-    "P10": (711,),
-    "P11": (305, 325, 523, 314,),
-    "Q": (4000, 602, 801,),
-    "W0": (404, 414, 513, 722, 900, 910, 920,),
-    "W1": (424, 504, 612, 623, 1000, 1010, 1020,),
-    "W2": (3003, 315, 811, 822, 1100, 4001, 1110, 1120,),
-    "I0": (405, 514, 524, 921,),
-    "I1": (415, 425, 603, 702, 712, 1021,),
-    "I2": (505, 723, 802, 624, 901, 911,),
-    "T0": (1001, 1011, 1101, 1111, 1121, 613, 515, 3004, 525, 823, 922, 812, 604, 713, 703, 625, 4002, 724, 803,),
-    "T1": (1022, 605, 902, 912, 725, 3005, 1122, 614, 714, 1002, 704, 1012, 804, 1102, 615, 1112, 715, 813, 824,),
-    "T2": (705, 805, 1023, 923, 913, 814, 903, 825, 4003, 1013, 1123, 1113, 914, 924, 1003, 904, 815, 1103, 1014,),
-    "T3": (1124, 1024, 1114, 4004, 1004, 915, 925, 1104, 905, 1015, 1125, 1025, 1115, 1005, 1105, 4005,),
+    "U0": (200, 210, 220, 300, 310,),
+    "U1": (1, 11, 320,),
+    "U2": (21, 101, 111, 121, 400, 410, 420, 500, 510, 520,),
+    "U3": (201, 211,),
+    "U4": (2, 12, 221,),
+    "U5": (301, 311,),
+    "U6": (22, 321, 102, 600, 610, 620, 700, 710, 720,),
+    "U7": (421, 112, 122,),
+    "L0": (3000,),
+    "L1": (202, 212, 800, 810, 820,),
+    "L2": (3, 222, 411,),
+    "P0": (13, 312, 521,),
+    "P1": (401, 23, 2000,),
+    "P2": (103, 302,),
+    "P3": (113, 123, 203, 322, 4, 3001,),
+    "P4": (14, 213, 223, 422, 511, 621,),
+    "P5": (412, 2001,),
+    "P6": (24, 104, 313, 522, 5, 501, 721,),
+    "P7": (15, 114, 124, 204, 402, 323, 3002,),
+    "P8": (214, 224, 303, 423, 601, 611,),
+    "P9": (25, 413, 821, 105, 2002,),
+    "P10": (115, 314, 512, 711,),
+    "P11": (125, 205, 523, 215, 622, 3003,),
+    "Q": (225, 324, 403, 4000,),
+    "W0": (304, 424, 502, 701, 900, 910, 920,),
+    "W1": (414, 315, 722, 1000, 1010, 1020, 2003,),
+    "W2": (602, 612, 1100, 1110, 1120,),
+    "I0": (325, 524, 404, 513, 822, 811, 921, 3004,),
+    "I1": (305, 425, 712,),
+    "I2": (415, 503, 623, 801, 1021, 4001,),
+    "T0": (901, 911, 1001, 1011, 1101, 1111, 1121, 514, 702, 723, 525, 405, 613, 603, 922, 823, 504, 713, 515, 812,
+        2004, 3005, 4002,),
+    "T1": (624, 1022, 802, 505, 912, 625, 1122, 614, 902, 604, 1012, 714, 1002, 615, 1112, 605, 715, 703, 1102,
+        724, 4003, 3006,),
+    "T2": (923, 824, 813, 704, 803, 1023, 1123, 725, 913, 814, 825, 903, 804, 705, 1013, 1003, 1113, 914, 924,
+        1103, 2005, 4004,),
+    "T3": (904, 815, 1124, 1024, 1014, 805, 1004, 1114, 1104, 915, 925, 905, 1125, 1025, 1015, 1005, 1115, 1105,
+        4005,),
 }
 
 
@@ -737,7 +780,7 @@
 
     def kernel(states_ref, grad_ref, logits_ref, sums_ref, small_ref, late_ref, got_ref, states_out, grad_out, logits_out, up, down,
                out, query, key, value, pool, query_bias, value_bias, out_bias, first_gain, first_shift, up_bias,
-               down_bias, second_gain, second_shift, pool_bias, class_weight, class_bias, loss, left, right, sem):
+               down_bias, second_gain, second_shift, pool_bias, class_weight, class_bias, loss, left, right, late_wide, sem):
         copies = [
             pltpu.make_async_copy(states_ref, states_out, sem.at[0]), pltpu.make_async_copy(grad_ref, grad_out, sem.at[1])]
         for copy in copies:
@@ -756,18 +799,20 @@
         def wide(k):
             return jnp.concatenate([got[:, k * lanes + j, :] for j in range(lanes)], 1)
 
-        lead, grad_pooled, pooled = wide(0), wide(1), wide(2)
-        grad_logits = got[:, 3 * lanes, :]
+        lead, grad_pooled = wide(0), wide(1)
         left[...] = lead.T
         right[...] = grad_pooled
         at = pl.ds(pl.multiple_of(head * half, half), half)
         pool[...] = matmul(
             left[pl.ds(pl.multiple_of(dp * block, 8), block), :].astype(BF16), right[:, at].astype(BF16))
         pool_bias[...] = jnp.sum(grad_pooled, 0)
-        class_weight[...] = tn(grad_logits.astype(BF16), pooled.astype(BF16))[0:classes, :]
-        class_bias[...] = jnp.sum(grad_logits, 0, keepdims=True)[:, 0:classes].reshape(classes)
-        query_bias[...] = late_ref[0:1, at].reshape(half)
-        value_bias[...] = late_ref[1:2, at].reshape(half)
+        for k in range(classes):
+            class_weight[k : k + 1, :] = small_ref[CLASS_ROWS[k] : CLASS_ROWS[k] + 1, :]
+        class_bias[...] = small_ref[LOSS : LOSS + 1, 128 : 128 + classes].reshape(classes)
+        for n in range(2):
+            late_wide[n : n + 1, :] = jnp.concatenate([late_ref[3 * n + t : 3 * n + t + 1, :] for t in range(3)], 1)
+        query_bias[...] = late_wide[0:1, at].reshape(half)
+        value_bias[...] = late_wide[1:2, at].reshape(half)
         for ref, row in ((out_bias, OUT_BIAS), (first_gain, FIRST_GAIN), (first_shift, FIRST_SHIFT),
                          (down_bias, DOWN_BIAS), (second_gain, SECOND_GAIN), (second_shift, SECOND_SHIFT)):
             ref[...] = small_ref[row, :]
@@ -795,7 +840,8 @@
         in_specs=[vmem] * 7,
         out_specs=[anywhere] * 2 + [vmem] * 20 + [pl.BlockSpec(memory_space=pltpu.SMEM)],
         scratch_shapes=[
-            pltpu.VMEM((width, devices), F32), pltpu.VMEM((devices, width), F32), pltpu.SemaphoreType.DMA((2,))],
+            pltpu.VMEM((width, devices), F32), pltpu.VMEM((devices, width), F32),
+            pltpu.VMEM((8, width), F32), pltpu.SemaphoreType.DMA((2,))],
         compiler_params=pltpu.CompilerParams(vmem_limit_bytes=VMEM_LIMIT),
         name="spread",
     )(states, input_grad, logits, sums, small, late, gathered)
@@ -943,7 +989,7 @@
     classes = class_weight.shape[1]
     direct = (
         (width // dp_size) % 16 == 0 and head_size == 2 and bits == 5 and hidden == 4 * width and rows == SEQ_LEN
-        and labels.shape[0] == 1
+        and labels.shape[0] == 1 and classes == len(CLASS_ROWS)
     )
     if not direct:
         return plain_body(*args)

time: 137 us -> 131 us (0.956)
  Pallas kernels: 135 us -> 129 us
    pallas_call x1, Pallas kernels: 100 us -> 96.6 us  [rest_of_layer(): pl.pallas_call(kernel, out_shape=[act, act, jax.ShapeDtypeStruct((1, clas...]
    pallas_call x1, Pallas kernels: 30.6 us -> 28.8 us  [attention_forward(): pl.pallas_call(kernel, out_shape=[act] * 4 + [jax.ShapeDtypeStruct((2 * p...]
where the time goes in v3:
time: 131 us
  Pallas kernels  129 us (98%)
  between operations  1.52 us (1%)
    pallas_call x1, Pallas kernels, rest_of_layer(): pl.pallas_call(kernel, out_shape=[act, act, jax.ShapeDtypeStruct((1, clas...  96.6 us
    pallas_call x1, Pallas kernels, attention_forward(): pl.pallas_call(kernel, out_shape=[act] * 4 + [jax.ShapeDtypeStruct((2 * p...  28.8 us
    pallas_call x1, Pallas kernels, spread(): pl.pallas_call(kernel, out_shape=[act, act, f32(1, classes), f32(block, t...  3.86 us

profile of v3, /device:TPU:0, one launch (start us, length us, event | category | flops | bytes accessed | tf_op | source)
XLA Modules:
  0.0 130.8 jit_solution(9370054339809558511)
XLA Ops:
  1.3 28.8 %attention_forward.1 = (bf16[512,768]{1,0:T(8,128)(2,1)}, bf16[512,768]{1,0:T(8,128)(2,1)}, bf16[512,768]{1,0:T(8,128)(2,1)}, bf16[512,768]{1,0:T(8,128)(2,1)}, ...) custom-call(s32[2]{0:T(128)} %lengths_ref.3, ...), custom_call_target="tpu_custom_call" | custom-call | tf_op jit(solution)/shard_map/attention_forward/pallas_call | solution.py:236
  30.1 96.6 %rest_of_layer.1 = (bf16[512,768]{1,0:T(8,128)(2,1)}, bf16[512,768]{1,0:T(8,128)(2,1)}, f32[1,3]{1,0:T(1,128)}, f32[36,48,128]{2,1,0:T(8,128)}, f32[16,768]{1,0:...) custom-call(s32[2]{0:T(128)} %lengths_ref.3, s32[1]{0:T(128)S(6)} %copy.46.labels_ref, ...), custom_call_target="tpu_custom_call" | custom-call | tf_op jit(solution)/shard_map/rest_of_layer/pallas_call | solution.py:674
  126.8 3.9 %spread.1 = (bf16[512,768]{1,0:T(8,128)(2,1)}, bf16[512,768]{1,0:T(8,128)(2,1)}, f32[1,3]{1,0:T(1,128)}, f32[48,1536]{1,0:T(8,128)}, f32[192,384]{1,0:T(8,128)},...) custom-call(bf16[512,768]{1,0:T(8,128)(2,1)} %get-tuple-element.69.s, ...), custom_call_target="tpu_custom_call" | custom-call | tf_op jit(solution)/shard_map/spread/pallas_call | solution.py:833

commit v4 on v3

--- a/solution.py
+++ b/solution.py
@@ -726,45 +726,41 @@
     "D0": (),
     "D1": (),
     "D2": (),
-    "D3": (0, 10, 20, 100, 110, 120,),
-    "U0": (200, 210, 220, 300, 310,),
-    "U1": (1, 11, 320,),
-    "U2": (21, 101, 111, 121, 400, 410, 420, 500, 510, 520,),
-    "U3": (201, 211,),
-    "U4": (2, 12, 221,),
-    "U5": (301, 311,),
-    "U6": (22, 321, 102, 600, 610, 620, 700, 710, 720,),
-    "U7": (421, 112, 122,),
-    "L0": (3000,),
-    "L1": (202, 212, 800, 810, 820,),
-    "L2": (3, 222, 411,),
-    "P0": (13, 312, 521,),
-    "P1": (401, 23, 2000,),
-    "P2": (103, 302,),
-    "P3": (113, 123, 203, 322, 4, 3001,),
-    "P4": (14, 213, 223, 422, 511, 621,),
-    "P5": (412, 2001,),
-    "P6": (24, 104, 313, 522, 5, 501, 721,),
-    "P7": (15, 114, 124, 204, 402, 323, 3002,),
-    "P8": (214, 224, 303, 423, 601, 611,),
-    "P9": (25, 413, 821, 105, 2002,),
-    "P10": (115, 314, 512, 711,),
-    "P11": (125, 205, 523, 215, 622, 3003,),
-    "Q": (225, 324, 403, 4000,),
-    "W0": (304, 424, 502, 701, 900, 910, 920,),
-    "W1": (414, 315, 722, 1000, 1010, 1020, 2003,),
-    "W2": (602, 612, 1100, 1110, 1120,),
-    "I0": (325, 524, 404, 513, 822, 811, 921, 3004,),
-    "I1": (305, 425, 712,),
-    "I2": (415, 503, 623, 801, 1021, 4001,),
-    "T0": (901, 911, 1001, 1011, 1101, 1111, 1121, 514, 702, 723, 525, 405, 613, 603, 922, 823, 504, 713, 515, 812,
-        2004, 3005, 4002,),
-    "T1": (624, 1022, 802, 505, 912, 625, 1122, 614, 902, 604, 1012, 714, 1002, 615, 1112, 605, 715, 703, 1102,
-        724, 4003, 3006,),
-    "T2": (923, 824, 813, 704, 803, 1023, 1123, 725, 913, 814, 825, 903, 804, 705, 1013, 1003, 1113, 914, 924,
-        1103, 2005, 4004,),
-    "T3": (904, 815, 1124, 1024, 1014, 805, 1004, 1114, 1104, 915, 925, 905, 1125, 1025, 1015, 1005, 1115, 1105,
-        4005,),
+    "D3": (0, 10, 20, 100, 110,),
+    "U0": (120, 200, 210, 220, 300,),
+    "U1": (1, 11, 21, 310, 320,),
+    "U2": (101, 111, 121, 400, 410, 420, 500, 510,),
+    "U3": (201, 211, 221, 520,),
+    "U4": (2, 12, 22, 311, 321,),
+    "U5": (112, 421,),
+    "U6": (102, 122, 212, 222, 521, 600, 610, 620, 700, 710,),
+    "U7": (202, 301, 720,),
+    "L0": (3, 23, 3000,),
+    "L1": (13, 322, 312, 113, 800, 810, 820,),
+    "L2": (411, 621,),
+    "P0": (422, 123,),
+    "P1": (103, 203, 223, 522, 401, 2000,),
+    "P2": (4, 14, 24, 114, 213, 323, 302, 721, 501, 511,),
+    "P3": (313, 3001,),
+    "P4": (104, 124, 224, 423, 412, 204, 611, 821,),
+    "P5": (5, 15, 214, 324, 303, 25, 523, 622, 2001,),
+    "P6": (115, 402, 601,),
+    "P7": (105, 125, 314, 424, 502, 512, 722, 225, 3002,),
+    "P8": (205, 215, 325, 524, 304, 413, 822, 711,),
+    "P9": (612, 701, 403, 623, 2002,),
+    "P10": (315, 425, 503, 602,),
+    "P11": (525, 414, 513, 305, 723, 801, 811, 3003,),
+    "Q": (404, 4000,),
+    "W0": (823, 900, 910, 920,),
+    "W1": (504, 624, 613, 712, 1000, 1010, 1020, 2003,),
+    "W2": (1100, 1110, 1120,),
+    "I0": (415, 514, 603, 702, 724, 901, 3004,),
+    "I1": (405, 911, 921, 812,),
+    "I2": (505, 614, 824, 802, 1001, 625, 1021, 4001,),
+    "T0": (1011, 1101, 1111, 1121, 604, 713, 703, 515, 725, 902, 912, 922, 615, 813, 825, 2004, 3005, 4002,),
+    "T1": (605, 803, 1022, 1002, 1012, 1122, 1102, 714, 1112, 704, 913, 814, 903, 804, 1023, 4003, 3006,),
+    "T2": (923, 715, 1013, 914, 705, 1003, 904, 815, 1113, 805, 1123, 924, 1014, 1103, 1004, 2005, 4004,),
+    "T3": (915, 1024, 1114, 905, 1124, 925, 1104, 1015, 1005, 1025, 1115, 1125, 1105, 4005,),
 }
 
 

time: 131 us -> 129 us (0.985)
  Pallas kernels: 129 us -> 127 us
    pallas_call x1, Pallas kernels: 96.6 us -> 94.2 us  [rest_of_layer(): pl.pallas_call(kernel, out_shape=[act, act, jax.ShapeDtypeStruct((1, clas...]
where the time goes in v4:
time: 129 us; the launch traced here: 128 us
  Pallas kernels  127 us (98%)
  between operations  1.52 us (1%)
    pallas_call x1, Pallas kernels, rest_of_layer(): pl.pallas_call(kernel, out_shape=[act, act, jax.ShapeDtypeStruct((1, clas...  94.2 us
    pallas_call x1, Pallas kernels, attention_forward(): pl.pallas_call(kernel, out_shape=[act] * 4 + [jax.ShapeDtypeStruct((2 * p...  28.8 us
    pallas_call x1, Pallas kernels, spread(): pl.pallas_call(kernel, out_shape=[act, act, f32(1, classes), f32(block, t...  3.86 us

profile of v4, /device:TPU:0, one launch (start us, length us, event | category | flops | bytes accessed | tf_op | source)
XLA Modules:
  0.0 128.5 jit_solution(4983500643713508207)
XLA Ops:
  1.3 28.8 %attention_forward.1 = (bf16[512,768]{1,0:T(8,128)(2,1)}, bf16[512,768]{1,0:T(8,128)(2,1)}, bf16[512,768]{1,0:T(8,128)(2,1)}, bf16[512,768]{1,0:T(8,128)(2,1)}, ...) custom-call(s32[2]{0:T(128)} %lengths_ref.3, ...), custom_call_target="tpu_custom_call" | custom-call | tf_op jit(solution)/shard_map/attention_forward/pallas_call | solution.py:236
  30.1 94.2 %rest_of_layer.1 = (bf16[512,768]{1,0:T(8,128)(2,1)}, bf16[512,768]{1,0:T(8,128)(2,1)}, f32[1,3]{1,0:T(1,128)}, f32[36,48,128]{2,1,0:T(8,128)}, f32[16,768]{1,0:...) custom-call(s32[2]{0:T(128)} %lengths_ref.3, s32[1]{0:T(128)S(6)} %copy.46.labels_ref, ...), custom_call_target="tpu_custom_call" | custom-call | tf_op jit(solution)/shard_map/rest_of_layer/pallas_call | solution.py:674
  124.4 3.9 %spread.1 = (bf16[512,768]{1,0:T(8,128)(2,1)}, bf16[512,768]{1,0:T(8,128)(2,1)}, f32[1,3]{1,0:T(1,128)}, f32[48,1536]{1,0:T(8,128)}, f32[192,384]{1,0:T(8,128)},...) custom-call(bf16[512,768]{1,0:T(8,128)(2,1)} %get-tuple-element.69.s, ...), custom_call_target="tpu_custom_call" | custom-call | tf_op jit(solution)/shard_map/spread/pallas_call | solution.py:829

commit v5 on v4

--- a/solution.py
+++ b/solution.py
@@ -144,6 +144,8 @@
         for j in range(3):
             mine = rows_of(x, z)
             start(j, 0, own_refs[j].at[mine, :], (mine, own), bits - 1)
+        far = rows_of(1 - x, 1 - z)
+        start(2, 3, own_refs[2].at[far, :], (far, own), bits - 1)
         for copy in bias_copies:
             copy.start()
 
@@ -159,19 +161,25 @@
 
         def stage_two(j):
             started[j, 1].wait_recv()
-            forward(j, 4, (rows_of(1 - x, z, 1), other), bit_z)
+            if j < 2:
+                forward(j, 4, (rows_of(1 - x, z, 1), other), bit_z)
             forward(j, 6, (rows_of(1 - x, z), other), 0)
             started[j, 2].wait_recv()
-            forward(j, 3, (rows_of(x, 1 - z, 0), other), bit_x)
+            if j < 2:
+                forward(j, 3, (rows_of(x, 1 - z, 0), other), bit_x)
             forward(j, 7, (rows_of(x, 1 - z), other), 0)
 
         def stage_three(j):
+            if j == 2:
+                started[j, 3].wait_recv()
+                forward(j, 8, (far, other), 0)
+                return
             for kind, lower in ((3, 0), (4, 1)):
                 started[j, kind].wait_recv()
                 forward(j, kind + 5, (rows_of(1 - x, 1 - z, lower), other), 0)
 
         def stage_four(j):
-            for kind in range(5, 10):
+            for kind in range(5, 10 if j < 2 else 9):
                 started[j, kind].wait_recv()
 
         def project(j, where, bias):

time: 129 us -> 126 us (0.977)
  Pallas kernels: 127 us -> 124 us
    pallas_call x1, Pallas kernels: 28.8 us -> 26.1 us  [attention_forward(): pl.pallas_call(kernel, out_shape=[act] * 4 + [jax.ShapeDtypeStruct((2 * p...]
where the time goes in v5:
time: 126 us
  Pallas kernels  124 us (98%)
  between operations  1.52 us (1%)
    pallas_call x1, Pallas kernels, rest_of_layer(): pl.pallas_call(kernel, out_shape=[act, act, jax.ShapeDtypeStruct((1, clas...  94.4 us
    pallas_call x1, Pallas kernels, attention_forward(): pl.pallas_call(kernel, out_shape=[act] * 4 + [jax.ShapeDtypeStruct((2 * p...  26.1 us
    pallas_call x1, Pallas kernels, spread(): pl.pallas_call(kernel, out_shape=[act, act, f32(1, classes), f32(block, t...  3.86 us

profile of v5, /device:TPU:0, one launch (start us, length us, event | category | flops | bytes accessed | tf_op | source)
XLA Modules:
  0.0 125.9 jit_solution(1231860810620579495)
XLA Ops:
  1.3 26.1 %attention_forward.1 = (bf16[512,768]{1,0:T(8,128)(2,1)}, bf16[512,768]{1,0:T(8,128)(2,1)}, bf16[512,768]{1,0:T(8,128)(2,1)}, bf16[512,768]{1,0:T(8,128)(2,1)}, ...) custom-call(s32[2]{0:T(128)} %lengths_ref.3, ...), custom_call_target="tpu_custom_call" | custom-call | tf_op jit(solution)/shard_map/attention_forward/pallas_call | solution.py:244
  27.4 94.4 %rest_of_layer.1 = (bf16[512,768]{1,0:T(8,128)(2,1)}, bf16[512,768]{1,0:T(8,128)(2,1)}, f32[1,3]{1,0:T(1,128)}, f32[36,48,128]{2,1,0:T(8,128)}, f32[16,768]{1,0:...) custom-call(s32[2]{0:T(128)} %lengths_ref.3, s32[1]{0:T(128)S(6)} %copy.46.labels_ref, ...), custom_call_target="tpu_custom_call" | custom-call | tf_op jit(solution)/shard_map/rest_of_layer/pallas_call | solution.py:682
  121.9 3.9 %spread.1 = (bf16[512,768]{1,0:T(8,128)(2,1)}, bf16[512,768]{1,0:T(8,128)(2,1)}, f32[1,3]{1,0:T(1,128)}, f32[48,1536]{1,0:T(8,128)}, f32[192,384]{1,0:T(8,128)},...) custom-call(bf16[512,768]{1,0:T(8,128)(2,1)} %get-tuple-element.69.s, ...), custom_call_target="tpu_custom_call" | custom-call | tf_op jit(solution)/shard_map/spread/pallas_call | solution.py:837
